TPU v7x, 128 devices: a whole 4x4x4 slice. The times are simulated.
128 devices in a mesh: fsdp: 64 (over z, x_hi, y, core), seq: 2 (over x_lo).
Axes of the slice: x: 4 (x_hi: 2, x_lo: 2; x = x_hi * 2 + x_lo), y: 4, z: 4, core: 2. Of those that a mesh axis runs over, the one named last changes fastest.
Arguments:
- tokens_in: bfloat16 [64, 256, 1024], P('fsdp', 'seq'), may hold values from -16 to 16
- noise_emb: bfloat16 [64, 1024], P('fsdp'), may hold values from -6 to 6
- text_emb: bfloat16 [64, 8, 768], P('fsdp'), may hold values from -16 to 16
- prompt_len: int32 [64], P('fsdp'), may hold values from 1 to 8, as said below
- mod_weight: bfloat16 [1024, 2048], P('fsdp'), may hold values from -0.09375 to 0.09375
- qkv_weight: bfloat16 [1024, 3, 1024], P('fsdp'), may hold values from -0.1875 to 0.1875
- proj_weight: bfloat16 [1024, 1024], P('fsdp'), may hold values from -1.5 to 1.5
- cq_weight: bfloat16 [1024, 1024], P('fsdp'), may hold values from -0.1875 to 0.1875
- text_weight: bfloat16 [768, 2, 1024], P('fsdp', None, 'seq'), may hold values from -0.21875 to 0.21875
- co_weight: bfloat16 [1024, 1024], P('fsdp'), may hold values from -0.375 to 0.375
- norm_gains: bfloat16 [2, 1024], P(None, 'fsdp'), may hold values from 0.099609375 to 1.8984375
- up_weight: bfloat16 [1024, 4096], P('fsdp'), may hold values from -0.1875 to 0.1875
- down_weight: bfloat16 [4096, 1024], P('fsdp'), may hold values from -0.09375 to 0.09375
- out_grad: bfloat16 [64, 256, 1024], P('fsdp', 'seq'), may hold values from -6 to 6
Outputs:
- block_out: bfloat16 [64, 256, 1024], P('fsdp', 'seq')
- tokens_grad: float32 [64, 256, 1024], P('fsdp', 'seq')
- noise_grad: float32 [64, 1024], P('fsdp')
- text_grad: float32 [64, 8, 768], P('fsdp')
- mod_wgrad: float32 [1024, 2048], P('fsdp')
- qkv_wgrad: float32 [1024, 3, 1024], P('fsdp')
- proj_wgrad: float32 [1024, 1024], P('fsdp')
- cq_wgrad: float32 [1024, 1024], P('fsdp')
- text_wgrad: float32 [768, 2, 1024], P('fsdp', None, 'seq')
- co_wgrad: float32 [1024, 1024], P('fsdp')
- gains_grad: float32 [2, 1024], P(None, 'fsdp')
- up_wgrad: float32 [1024, 4096], P('fsdp')
- down_wgrad: float32 [4096, 1024], P('fsdp')
Inputs may be any that keep to these rules, and one draw needn't show every extreme that they name: Image i uses its first prompt_len[i] text positions as keys; in every draw some image uses all 8.
All inputs are finite; a program needn't handle non-finite values.
Results may differ from a plain program's by a relative error of at most 0.018.
Values may be sent and summed in bfloat16 or wider, within the bound.
No kernel may reach another device: no remote copies, remote signals or barrier semaphores. Data moves between devices by JAX's collectives and lax.ppermute only.
A program may use at most 192 MiB of HBM per device.

v0:
```python
from functools import partial

import jax
import jax.numpy as jnp
from jax import lax
from jax.sharding import PartitionSpec as P

HEAD_DIM = 64


EPSILON = 1e-06
HIGHEST_PREC = lax.Precision.HIGHEST
NEG_LARGE = -1e30


def rms_norm(tensor):
    return tensor * lax.rsqrt(jnp.mean(tensor * tensor, axis=-1, keepdims=True) + EPSILON)


def gained_norm(tensor, gain_vec):
    return rms_norm(tensor) * gain_vec


def modulated_norm(tensor, modulation):
    model_width = tensor.shape[-1]
    return (
        rms_norm(tensor) * (1.0 + modulation[:, None, :model_width])
        + modulation[:, None, model_width:]
    )


def split_heads(tensor):
    return tensor.reshape(tensor.shape[:-1] + (tensor.shape[-1] // HEAD_DIM, HEAD_DIM))


def score_block(queries, keys_all, usable):
    scores = jnp.einsum(
        "iqhd,ikhd->ihqk", queries, keys_all, preferred_element_type=jnp.float32
    ) * HEAD_DIM ** (-0.5)
    if usable is None:
        return scores
    return jnp.where(usable[:, None, None, :], scores, NEG_LARGE)


def attend_forward(queries, keys_all, values_all, usable):
    scores = score_block(queries, keys_all, usable)
    row_max = jnp.max(scores, axis=-1, keepdims=True)
    log_total = row_max + jnp.log(jnp.sum(jnp.exp(scores - row_max), axis=-1, keepdims=True))
    softmax_w = jnp.exp(scores - log_total).astype(jnp.bfloat16)
    mixed_heads = jnp.einsum(
        "ihqk,ikhd->iqhd", softmax_w, values_all, preferred_element_type=jnp.float32
    )
    return (mixed_heads, log_total)


def attend_backward(queries, keys_all, values_all, usable, log_total, mixed_grad):
    factor = HEAD_DIM ** (-0.5)
    scores = score_block(queries, keys_all, usable)
    softmax_w = jnp.exp(scores - log_total)
    softmax_low = softmax_w.astype(jnp.bfloat16)
    prob_grad = jnp.einsum(
        "iqhd,ikhd->ihqk", mixed_grad, values_all, preferred_element_type=jnp.float32
    )
    inner_sum = jnp.sum(softmax_w * prob_grad, axis=-1, keepdims=True)
    score_grad = (softmax_w * (prob_grad - inner_sum)).astype(jnp.bfloat16)
    query_grad = (
        jnp.einsum("ihqk,ikhd->iqhd", score_grad, keys_all, preferred_element_type=jnp.float32)
        * factor
    )
    key_grad = (
        jnp.einsum("ihqk,iqhd->ikhd", score_grad, queries, preferred_element_type=jnp.float32)
        * factor
    )
    value_grad = jnp.einsum(
        "ihqk,iqhd->ikhd", softmax_low, mixed_grad, preferred_element_type=jnp.float32
    )
    return (query_grad, key_grad, value_grad)


def project(left, right):
    return jnp.einsum("itd,de->ite", left, right, preferred_element_type=jnp.float32)


def project_back(left, right):
    return jnp.einsum("ite,de->itd", left, right, preferred_element_type=jnp.float32)


def outer_sum(left, right):
    return jnp.einsum("itd,ite->de", left, right, preferred_element_type=jnp.float32)


def per_device(
    tokens_in,
    noise_emb,
    text_emb,
    prompt_len,
    mod_weight,
    qkv_weight,
    proj_weight,
    cq_weight,
    text_weight,
    co_weight,
    norm_gains,
    up_weight,
    down_weight,
    out_grad,
):
    images, tok_rows, model_width = tokens_in.shape
    txt_rows = text_emb.shape[1]
    gathered = (
        lax.all_gather(mod_weight, "fsdp", axis=0, tiled=True),
        lax.all_gather(qkv_weight, "fsdp", axis=0, tiled=True),
        lax.all_gather(proj_weight, "fsdp", axis=0, tiled=True),
        lax.all_gather(cq_weight, "fsdp", axis=0, tiled=True),
        lax.all_gather(text_weight, "fsdp", axis=0, tiled=True),
        lax.all_gather(co_weight, "fsdp", axis=0, tiled=True),
        lax.all_gather(norm_gains, "fsdp", axis=1, tiled=True),
    )
    mod_full, qkv_full, proj_full, cq_full, text_full, co_full, gains_full = gathered
    up_full, down_full = (
        lax.all_gather(up_weight, "fsdp", axis=0, tiled=True),
        lax.all_gather(down_weight, "fsdp", axis=0, tiled=True),
    )
    gain_two = gains_full[0].astype(jnp.float32)
    gain_three = gains_full[1].astype(jnp.float32)
    tokens = tokens_in.astype(jnp.float32)
    modulation = jnp.dot(noise_emb, mod_full, preferred_element_type=jnp.float32)
    normed_one = modulated_norm(tokens, modulation).astype(jnp.bfloat16)
    qkv_local = jnp.einsum(
        "itd,dcn->itcn", normed_one, qkv_full, preferred_element_type=jnp.float32
    ).astype(jnp.bfloat16)
    queries = split_heads(qkv_local[:, :, 0])
    kv_all = lax.all_gather(qkv_local[:, :, 1:], "seq", axis=1, tiled=True)
    keys_all = split_heads(kv_all[:, :, 0])
    values_all = split_heads(kv_all[:, :, 1])
    mixed_heads, self_lse = attend_forward(queries, keys_all, values_all, None)
    attended = mixed_heads.reshape(images, tok_rows, model_width).astype(jnp.bfloat16)
    after_self = tokens + project(attended, proj_full)
    normed_two = gained_norm(after_self, gain_two).astype(jnp.bfloat16)
    cross_q = split_heads(project(normed_two, cq_full).astype(jnp.bfloat16))
    text_local = jnp.einsum(
        "ijt,tcn->ijcn", text_emb, text_full, preferred_element_type=jnp.float32
    ).astype(jnp.bfloat16)
    text_kv = lax.all_gather(text_local, "seq", axis=3, tiled=True)
    text_keys = split_heads(text_kv[:, :, 0])
    text_vals = split_heads(text_kv[:, :, 1])
    usable = jnp.arange(txt_rows, dtype=jnp.int32)[None, :] < prompt_len[:, None]
    cross_heads, cross_lse = attend_forward(cross_q, text_keys, text_vals, usable)
    cross_att = cross_heads.reshape(images, tok_rows, model_width).astype(jnp.bfloat16)
    after_cross = after_self + project(cross_att, co_full)
    normed_three = gained_norm(after_cross, gain_three).astype(jnp.bfloat16)
    pre_act = project(normed_three, up_full)
    activated = jax.nn.gelu(pre_act, approximate=True).astype(jnp.bfloat16)
    block_out = (after_cross + project(activated, down_full)).astype(jnp.bfloat16)
    up_back, down_back = (
        lax.all_gather(up_weight, "fsdp", axis=0, tiled=True),
        lax.all_gather(down_weight, "fsdp", axis=0, tiled=True),
    )
    down_wfull = outer_sum(activated, out_grad)
    act_grad = project_back(out_grad, down_back)
    unused_out, gelu_back = jax.vjp(partial(jax.nn.gelu, approximate=True), pre_act)
    pre_grad = gelu_back(act_grad)[0].astype(jnp.bfloat16)
    up_wfull = outer_sum(normed_three, pre_grad)
    three_grad = project_back(pre_grad, up_back)
    up_wgrad, down_wgrad = (
        lax.psum_scatter(up_wfull, "fsdp", scatter_dimension=0, tiled=True),
        lax.psum_scatter(down_wfull, "fsdp", scatter_dimension=0, tiled=True),
    )
    unused_three, norm_back_three = jax.vjp(gained_norm, after_cross, gain_three)
    cross_tok_grad, gain_three_grad = norm_back_three(three_grad)
    cross_res_grad = out_grad.astype(jnp.float32) + cross_tok_grad
    cross_out_grad = cross_res_grad.astype(jnp.bfloat16)
    co_wfull = outer_sum(cross_att, cross_out_grad)
    cross_att_grad = project_back(cross_out_grad, co_full).astype(jnp.bfloat16)
    cq_heads_grad, text_key_grad, text_val_grad = attend_backward(
        cross_q, text_keys, text_vals, usable, cross_lse, split_heads(cross_att_grad)
    )
    text_kv_sum = jnp.stack(
        (
            text_key_grad.reshape(images, txt_rows, model_width),
            text_val_grad.reshape(images, txt_rows, model_width),
        ),
        axis=2,
    )
    text_kv_grad = lax.psum_scatter(
        text_kv_sum.astype(jnp.bfloat16), "seq", scatter_dimension=3, tiled=True
    )
    text_wfull = jnp.einsum(
        "ijt,ijcn->tcn", text_emb, text_kv_grad, preferred_element_type=jnp.float32
    )
    text_part = jnp.einsum(
        "ijcn,tcn->ijt", text_kv_grad, text_full, preferred_element_type=jnp.float32
    )
    cross_q_grad = cq_heads_grad.reshape(images, tok_rows, model_width).astype(jnp.bfloat16)
    cq_wfull = outer_sum(normed_two, cross_q_grad)
    two_grad = project_back(cross_q_grad, cq_full)
    unused_two, norm_back_two = jax.vjp(gained_norm, after_self, gain_two)
    self_tok_grad, gain_two_grad = norm_back_two(two_grad)
    self_res_grad = cross_res_grad + self_tok_grad
    proj_out_grad = self_res_grad.astype(jnp.bfloat16)
    proj_wfull = outer_sum(attended, proj_out_grad)
    attended_grad = project_back(proj_out_grad, proj_full).astype(jnp.bfloat16)
    query_grad, key_grad, value_grad = attend_backward(
        queries, keys_all, values_all, None, self_lse, split_heads(attended_grad)
    )
    kv_sum = jnp.stack(
        (key_grad.reshape(images, -1, model_width), value_grad.reshape(images, -1, model_width)),
        axis=2,
    )
    kv_grad = lax.psum_scatter(kv_sum.astype(jnp.bfloat16), "seq", scatter_dimension=1, tiled=True)
    qkv_grad = jnp.concatenate(
        (query_grad.reshape(images, tok_rows, 1, model_width).astype(jnp.bfloat16), kv_grad), axis=2
    )
    qkv_wfull = jnp.einsum(
        "itd,itcn->dcn", normed_one, qkv_grad, preferred_element_type=jnp.float32
    )
    one_grad = jnp.einsum("itcn,dcn->itd", qkv_grad, qkv_full, preferred_element_type=jnp.float32)
    unused_one, mod_back = jax.vjp(modulated_norm, tokens, modulation)
    input_part, mod_grad = mod_back(one_grad)
    tokens_grad = self_res_grad + input_part
    mod_wfull = jnp.dot(noise_emb.astype(jnp.float32).T, mod_grad, precision=HIGHEST_PREC)
    noise_part = jnp.dot(mod_grad, mod_full.astype(jnp.float32).T, precision=HIGHEST_PREC)
    gains_wfull = jnp.stack((gain_two_grad, gain_three_grad), axis=0)
    shards = (
        lax.psum_scatter(mod_wfull, "fsdp", scatter_dimension=0, tiled=True),
        lax.psum_scatter(qkv_wfull, "fsdp", scatter_dimension=0, tiled=True),
        lax.psum_scatter(proj_wfull, "fsdp", scatter_dimension=0, tiled=True),
        lax.psum_scatter(cq_wfull, "fsdp", scatter_dimension=0, tiled=True),
        lax.psum_scatter(text_wfull, "fsdp", scatter_dimension=0, tiled=True),
        lax.psum_scatter(co_wfull, "fsdp", scatter_dimension=0, tiled=True),
        lax.psum_scatter(gains_wfull, "fsdp", scatter_dimension=1, tiled=True),
    )
    mod_shard, qkv_shard, proj_shard, cq_shard, text_wgrad, co_shard, gains_shard = shards
    summed = (
        lax.psum(mod_shard.astype(jnp.bfloat16), "seq").astype(jnp.float32),
        lax.psum(qkv_shard.astype(jnp.bfloat16), "seq").astype(jnp.float32),
        lax.psum(proj_shard.astype(jnp.bfloat16), "seq").astype(jnp.float32),
        lax.psum(cq_shard.astype(jnp.bfloat16), "seq").astype(jnp.float32),
        lax.psum(co_shard.astype(jnp.bfloat16), "seq").astype(jnp.float32),
        lax.psum(gains_shard.astype(jnp.bfloat16), "seq").astype(jnp.float32),
        lax.psum(up_wgrad.astype(jnp.bfloat16), "seq").astype(jnp.float32),
        lax.psum(down_wgrad.astype(jnp.bfloat16), "seq").astype(jnp.float32),
        lax.psum(text_part.astype(jnp.bfloat16), "seq").astype(jnp.float32),
        lax.psum(noise_part.astype(jnp.bfloat16), "seq").astype(jnp.float32),
    )
    return (
        block_out,
        tokens_grad,
        summed[9],
        summed[8],
        summed[0],
        summed[1],
        summed[2],
        summed[3],
        text_wgrad,
        summed[4],
        summed[5],
        summed[6],
        summed[7],
    )


def solution(mesh):
    in_specs = (
        P("fsdp", "seq", None),
        P("fsdp", None),
        P("fsdp", None, None),
        P("fsdp"),
        P("fsdp", None),
        P("fsdp", None, None),
        P("fsdp", None),
        P("fsdp", None),
        P("fsdp", None, "seq"),
        P("fsdp", None),
        P(None, "fsdp"),
        P("fsdp", None),
        P("fsdp", None),
        P("fsdp", "seq", None),
    )
    out_specs = (
        P("fsdp", "seq", None),
        P("fsdp", "seq", None),
        P("fsdp", None),
        P("fsdp", None, None),
        P("fsdp", None),
        P("fsdp", None, None),
        P("fsdp", None),
        P("fsdp", None),
        P("fsdp", None, "seq"),
        P("fsdp", None),
        P(None, "fsdp"),
        P("fsdp", None),
        P("fsdp", None),
    )
    return jax.shard_map(
        per_device, mesh=mesh, in_specs=in_specs, out_specs=out_specs, check_vma=False
    )
```

profile of v0, /device:TPU:1, one launch (start us, length us, event | category | flops | bytes accessed | tf_op | source)
XLA Modules:
  0.0 4180.3 jit_solution(18347450597523893457)
XLA Ops:
  10.6 76.4 %all-gather.12.cloned.1.call-done = bf16[1024,2048]{1,0:T(8,128)(2,1)} async-done(((bf16[16,2048]{1,0:T(8,128)(2,1)}), bf16[1024,2048]{1,0:T(8,128)(2,1)}) %all-gather.12.cloned.1.call-update) | async-done | bytes 4194320 | tf_op jit(solution)/shard_map/all_gather | solution.py:111
  89.9 75.4 %all-gather.14.cloned.1.call-done = bf16[1024,3,1024]{2,0,1:T(8,128)(2,1)} async-done(((bf16[16,3,1024]{2,0,1:T(8,128)(2,1)}), bf16[1024,3,1024]{2,0,1:T(8,128)(2,1)}) %all-gather.14.cloned.1.call-update) | async-done | bytes 6291472 | tf_op jit(solution)/shard_map/all_gather | solution.py:112
  173.4 92.2 %all-gather.1 = bf16[64,16,2]{1,2,0:T(2,128)(2,1)S(1)} all-gather(bf16[1,16,2]{1,2,0:T(2,128)(2,1)S(1)} %bitcast.280), channel_id=1, replica_groups=mesh['fsdp'=64,'seq'=2] {'fsdp'}, dimensions={0}, use_global_device_ids=true | all-gather | bytes 4160 | tf_op jit(solution)/shard_map/all_gather | solution.py:117
  278.0 51.5 %all-gather.18.cloned.1.call-done = bf16[1024,1024]{1,0:T(8,128)(2,1)} async-done(((bf16[16,1024]{1,0:T(8,128)(2,1)}), bf16[1024,1024]{1,0:T(8,128)(2,1)}) %all-gather.18.cloned.1.call-update) | async-done | bytes 2097168 | tf_op jit(solution)/shard_map/all_gather | solution.py:113
  331.7 66.1 %all-gather.22.cloned.1.call-done = bf16[1024,1024]{1,0:T(8,128)(2,1)} async-done(((bf16[16,1024]{1,0:T(8,128)(2,1)}), bf16[1024,1024]{1,0:T(8,128)(2,1)}) %all-gather.22.cloned.1.call-update) | async-done | bytes 2097168 | tf_op jit(solution)/shard_map/all_gather | solution.py:114
  402.1 64.2 %all-gather.24.cloned.1.call-done = bf16[1024,1024]{1,0:T(8,128)(2,1)} async-done(((bf16[16,1024]{1,0:T(8,128)(2,1)}), bf16[1024,1024]{1,0:T(8,128)(2,1)}) %all-gather.24.cloned.1.call-update) | async-done | bytes 2097168 | tf_op jit(solution)/shard_map/all_gather | solution.py:116
  469.6 78.4 %all-gather.26.cloned.1.call-done = bf16[1024,4096]{1,0:T(8,128)(2,1)} async-done(((bf16[16,4096]{1,0:T(8,128)(2,1)}), bf16[1024,4096]{1,0:T(8,128)(2,1)}) %all-gather.26.cloned.1.call-update) | async-done | bytes 8388624 | tf_op jit(solution)/shard_map/all_gather | solution.py:121
  554.1 77.5 %all-gather.28.cloned.1.call-done = bf16[4096,1024]{1,0:T(8,128)(2,1)} async-done(((bf16[64,1024]{1,0:T(8,128)(2,1)}), bf16[4096,1024]{1,0:T(8,128)(2,1)}) %all-gather.28.cloned.1.call-update) | async-done | bytes 8388624 | tf_op jit(solution)/shard_map/all_gather | solution.py:122
  631.7 7.8 fusion.6
  684.4 6.3 reduce-scatter.13.cloned.1.call-done
  701.7 6.4 fusion.50
  709.4 8.2 fusion.98
  719.2 9.1 fusion.61
  739.1 296.4 %reduce-scatter.31.cloned.1.call-done = f32[16,2]{1,0:T(8,128)} async-done(((f32[1024,2]{1,0:T(8,128)}), f32[16,2]{1,0:T(8,128)}) %reduce-scatter.31.cloned.1.call-update) | async-done | bytes 144
  1045.5 325.3 %reduce-scatter.21.cloned.1.call-done = f32[16,1024]{1,0:T(8,128)} async-done(((f32[1024,1024]{1,0:T(8,128)}), f32[16,1024]{1,0:T(8,128)}) %reduce-scatter.21.cloned.1.call-update) | async-done | bytes 65552 | tf_op jit(solution)/shard_map/reduce_scatter | solution.py:227
  1372.2 333.9 %reduce-scatter.23.cloned.1.call-done = f32[16,1024]{1,0:T(8,128)} async-done(((f32[1024,1024]{1,0:T(8,128)}), f32[16,1024]{1,0:T(8,128)}) %reduce-scatter.23.cloned.1.call-update) | async-done | bytes 65552 | tf_op jit(solution)/shard_map/reduce_scatter | solution.py:228
  1707.6 333.8 %reduce-scatter.25.cloned.1.call-done = f32[16,1024]{1,0:T(8,128)} async-done(((f32[1024,1024]{1,0:T(8,128)}), f32[16,1024]{1,0:T(8,128)}) %reduce-scatter.25.cloned.1.call-update) | async-done | bytes 65552 | tf_op jit(solution)/shard_map/reduce_scatter | solution.py:230
  2048.7 335.5 %reduce-scatter.17.cloned.1.call-done = f32[16,2048]{1,0:T(8,128)} async-done(((f32[1024,2048]{1,0:T(8,128)}), f32[16,2048]{1,0:T(8,128)}) %reduce-scatter.17.cloned.1.call-update) | async-done | bytes 131088 | tf_op jit(solution)/shard_map/reduce_scatter | solution.py:225
  2385.8 348.1 %reduce-scatter.19.cloned.1.call-done = f32[16,3,1024]{2,0,1:T(8,128)} async-done(((f32[1024,3,1024]{2,0,1:T(8,128)}), f32[16,3,1024]{2,0,1:T(8,128)}) %reduce-scatter.19.cloned.1.call-update) | async-done | bytes 196624 | tf_op jit(solution)/shard_map/reduce_scatter | solution.py:226
  2735.5 355.2 %reduce-scatter.27.cloned.1.call-done = f32[16,4096]{1,0:T(8,128)} async-done(((f32[1024,4096]{1,0:T(8,128)}), f32[16,4096]{1,0:T(8,128)}) %reduce-scatter.27.cloned.1.call-update) | async-done | bytes 262160 | tf_op jit(solution)/shard_map/reduce_scatter | solution.py:166
  3092.4 355.5 %reduce-scatter.29.cloned.1.call-done = f32[64,1024]{1,0:T(8,128)} async-done(((f32[4096,1024]{1,0:T(8,128)}), f32[64,1024]{1,0:T(8,128)}) %reduce-scatter.29.cloned.1.call-update) | async-done | bytes 262160 | tf_op jit(solution)/shard_map/reduce_scatter | solution.py:167
  3451.5 643.4 %all-reduce.9.cloned.1.call-done = f32[768,2,512]{2,1,0:T(2,128)} async-done(((f32[768,2,512]{2,1,0:T(2,128)}), f32[768,2,512]{2,1,0:T(2,128)}) %all-reduce.9.cloned.1.call-update) | async-done | bytes 3145744
  4096.4 31.5 all-reduce.11.cloned.1.call-done
  4135.9 30.7 all-reduce.13.cloned.1.call-done
  (277 shorter events, 154.3 us)
Async XLA Ops:
  7.2 79.8 %all-gather.12.cloned.1.call-start = ((), (), s32[]{:S(2)}) async-start(), calls=%async_computation.10 | async-start | bytes 4259840 | tf_op jit(solution)/shard_map/all_gather | solution.py:111
  7.9 157.3 %all-gather.14.cloned.1.call-start = ((), (), s32[]{:S(2)}) async-start(), calls=%async_computation.11 | async-start | bytes 6389760 | tf_op jit(solution)/shard_map/all_gather | solution.py:112
  8.7 258.3 %all-gather.20.cloned.1.call-start = ((), (), s32[]{:S(2)}) async-start(), calls=%async_computation.14 | async-start | bytes 1597440 | tf_op jit(solution)/shard_map/all_gather | solution.py:115
  9.4 263.8 %all-gather.16.cloned.1.call-start = ((), (), s32[]{:S(2)}) async-start(), calls=%async_computation.12 | async-start | bytes 1572864 | tf_op jit(solution)/shard_map/all_gather | solution.py:133
  170.0 159.5 %all-gather.18.cloned.1.call-start = ((), (), s32[]{:S(2)}) async-start(), calls=%async_computation.13 | async-start | bytes 2129920 | tf_op jit(solution)/shard_map/all_gather | solution.py:113
  170.6 227.3 %all-gather.22.cloned.1.call-start = ((), (), s32[]{:S(2)}) async-start(), calls=%async_computation.15 | async-start | bytes 2129920 | tf_op jit(solution)/shard_map/all_gather | solution.py:114
  171.2 295.2 %all-gather.24.cloned.1.call-start = ((), (), s32[]{:S(2)}) async-start(), calls=%async_computation.16 | async-start | bytes 2129920 | tf_op jit(solution)/shard_map/all_gather | solution.py:116
  171.9 376.2 %all-gather.26.cloned.1.call-start = ((), (), s32[]{:S(2)}) async-start(), calls=%async_computation.17 | async-start | bytes 8519680 | tf_op jit(solution)/shard_map/all_gather | solution.py:121
  172.7 459.0 %all-gather.28.cloned.1.call-start = ((), (), s32[]{:S(2)}) async-start(), calls=%async_computation.18 | async-start | bytes 8519680 | tf_op jit(solution)/shard_map/all_gather | solution.py:122
  173.4 517.3 %reduce-scatter.13.cloned.1.call-start = ((), (), s32[]{:S(2)}) async-start(), calls=%async_computation.19 | async-start | bytes 1572864 | tf_op jit(solution)/shard_map/reduce_scatter | solution.py:210
  669.3 59.1 %reduce-scatter.15.cloned.1.call-start = ((), (), s32[]{:S(2)}) async-start(), calls=%async_computation.20 | async-start | bytes 49152 | tf_op jit(solution)/shard_map/reduce_scatter | solution.py:185
  670.8 364.7 %reduce-scatter.31.cloned.1.call-start = ((), (), s32[]{:S(2)}) async-start(), calls=%async_computation.28 | async-start | bytes 532480
  671.9 698.8 %reduce-scatter.21.cloned.1.call-start = ((), (), s32[]{:S(2)}) async-start(), calls=%async_computation.23 | async-start | bytes 4259840 | tf_op jit(solution)/shard_map/reduce_scatter | solution.py:227
  674.7 1031.4 %reduce-scatter.23.cloned.1.call-start = ((), (), s32[]{:S(2)}) async-start(), calls=%async_computation.24 | async-start | bytes 4259840 | tf_op jit(solution)/shard_map/reduce_scatter | solution.py:228
  678.5 1363.0 %reduce-scatter.25.cloned.1.call-start = ((), (), s32[]{:S(2)}) async-start(), calls=%async_computation.25 | async-start | bytes 4259840 | tf_op jit(solution)/shard_map/reduce_scatter | solution.py:230
  682.4 1701.9 %reduce-scatter.17.cloned.1.call-start = ((), (), s32[]{:S(2)}) async-start(), calls=%async_computation.21 | async-start | bytes 8519680 | tf_op jit(solution)/shard_map/reduce_scatter | solution.py:225
  700.7 2033.2 %reduce-scatter.19.cloned.1.call-start = ((), (), s32[]{:S(2)}) async-start(), calls=%async_computation.22 | async-start | bytes 12779520 | tf_op jit(solution)/shard_map/reduce_scatter | solution.py:226
  708.2 2382.6 %reduce-scatter.27.cloned.1.call-start = ((), (), s32[]{:S(2)}) async-start(), calls=%async_computation.26 | async-start | bytes 17039360 | tf_op jit(solution)/shard_map/reduce_scatter | solution.py:166
  717.6 2730.2 %reduce-scatter.29.cloned.1.call-start = ((), (), s32[]{:S(2)}) async-start(), calls=%async_computation.27 | async-start | bytes 17039360 | tf_op jit(solution)/shard_map/reduce_scatter | solution.py:167
  728.4 3366.6 %all-reduce.9.cloned.1.call-start = ((), (), s32[]{:S(2)}) async-start(), calls=%async_computation.29 | async-start | bytes 6291456
  737.2 299.6 %copy-start.40 = (bf16[1,8,2,512]{3,1,2,0:T(8,128)(2,1)S(1)}, bf16[1,8,2,512]{3,1,2,0:T(8,128)(2,1)}, u32[]{:S(2)}) copy-start(bf16[1,8,2,512]{3,1,2,0:T(8,128)(2,1)} %reduce-scatter.15.cloned.1.call-done) | copy-start | bytes 49156
  737.2 3390.7 %all-reduce.11.cloned.1.call-start = ((), (), s32[]{:S(2)}) async-start(), calls=%async_computation.30 | async-start | bytes 230400 | tf_op jit(solution)/shard_map/psum | solution.py:244
  2042.9 1406.5 %copy-start.57 = (f32[128]{0:T(128)S(1)}, f32[128]{0:T(128)}, u32[]{:S(2)}) copy-start(f32[128]{0:T(128)} %copy-done.56) | copy-start | bytes 1540
  2043.0 2123.7 %all-reduce.13.cloned.1.call-start = ((), (), s32[]{:S(2)}) async-start(), calls=%async_computation.31 | async-start | bytes 851968 | tf_op jit(solution)/shard_map/psum | solution.py:235
  (61 other events, 1517.3 us)
Sparse Core Ops, SparseCore 0:
  11.4 75.5 all-gather.11
  90.4 74.8 all-gather.13
  168.4 65.3 all-gather.19
  235.9 20.4 all-gather.15
  259.5 69.9 all-gather.17
  332.6 65.1 all-gather.21
  401.1 65.1 all-gather.23
  469.5 78.4 all-gather.25
  551.3 80.3 all-gather.27
  669.4 21.1 reduce-scatter.12
  693.6 12.7 reduce-scatter.14
  708.8 326.6 reduce-scatter.30
  1037.9 332.8 reduce-scatter.20
  1373.1 332.9 reduce-scatter.22
  1708.4 333.0 reduce-scatter.24
  2043.8 340.4 reduce-scatter.16
  2386.7 347.2 reduce-scatter.18
  2736.3 354.3 reduce-scatter.26
  3093.3 354.5 reduce-scatter.28
  3450.3 644.6 all-reduce.8
  4098.9 28.9 all-reduce.10
  4131.8 34.8 all-reduce.12
where the time goes:
time: 4190 us; the launch traced here: 4180 us
  waiting for transfers between devices  3890 us (93%)
  matrix products  105 us (3%)
  blocking collectives  95.6 us (2%)
    unnamed x24, waiting for transfers between devices  945 us
    reduce_scatter x1, waiting for transfers between devices, per_device(): lax.psum_scatter(down_wfull, 'fsdp', scatter_dimension=0, tiled=True)  355 us
    reduce_scatter x1, waiting for transfers between devices, per_device(): lax.psum_scatter(up_wfull, 'fsdp', scatter_dimension=0, tiled=True)  355 us
    reduce_scatter x1, waiting for transfers between devices, per_device(): lax.psum_scatter(qkv_wfull, 'fsdp', scatter_dimension=0, tiled=True)  348 us
    reduce_scatter x1, waiting for transfers between devices, per_device(): lax.psum_scatter(mod_wfull, 'fsdp', scatter_dimension=0, tiled=True)  336 us
    reduce_scatter x1, waiting for transfers between devices, per_device(): lax.psum_scatter(cq_wfull, 'fsdp', scatter_dimension=0, tiled=True)  334 us
    reduce_scatter x1, waiting for transfers between devices, per_device(): lax.psum_scatter(co_wfull, 'fsdp', scatter_dimension=0, tiled=True)  334 us
    reduce_scatter x1, waiting for transfers between devices, per_device(): lax.psum_scatter(proj_wfull, 'fsdp', scatter_dimension=0, tiled=True)  325 us
  transfers between devices with their start and end apart: 22, of which 19 were waited for; matrix products, arithmetic and copies ran while one was open for 3% of the time, Pallas kernels for 0%

commit v1 on v0

v1 whole, which is shorter than its diff:
```python
from functools import partial

import jax
import jax.numpy as jnp
from jax import lax
from jax.sharding import Mesh
from jax.sharding import PartitionSpec as P

HEAD_DIM = 64
EPSILON = 1e-06
HIGHEST_PREC = lax.Precision.HIGHEST
NEG_LARGE = -1e30
BF = jnp.bfloat16
F32 = jnp.float32

AXES = ("z", "xh", "y", "core", "xl")
SIZES = (4, 2, 4, 2, 2)
FSDP = ("z", "xh", "y", "core")
RING_X = ("xh", "xl")

D = 1024
FF = 4096
TEXT_W = 768
TXT = 8
CHIPS = 32

C_MOD, C_QKV, C_CQ, C_TEXT, C_PROJ, C_CO = 1024, 1536, 512, 512, 512, 512
TEXT_COLS = (C_MOD + C_QKV + C_CQ, C_MOD + C_QKV + C_CQ + C_TEXT)
C_UP, C_DOWN = 2048, 2048


def rms_norm(tensor):
    return tensor * lax.rsqrt(jnp.mean(tensor * tensor, axis=-1, keepdims=True) + EPSILON)


def gained_norm(tensor, gain_vec):
    return rms_norm(tensor) * gain_vec


def modulated_norm(tensor, scale, shift):
    return rms_norm(tensor) * (1.0 + scale[:, None, :]) + shift[:, None, :]


def split_heads(tensor):
    return tensor.reshape(tensor.shape[:-1] + (tensor.shape[-1] // HEAD_DIM, HEAD_DIM))


def score_block(queries, keys_all, usable):
    scores = jnp.einsum(
        "iqhd,ikhd->ihqk", queries, keys_all, preferred_element_type=F32
    ) * HEAD_DIM ** (-0.5)
    if usable is None:
        return scores
    return jnp.where(usable[:, None, None, :], scores, NEG_LARGE)


def attend_forward(queries, keys_all, values_all, usable):
    scores = score_block(queries, keys_all, usable)
    row_max = jnp.max(scores, axis=-1, keepdims=True)
    log_total = row_max + jnp.log(jnp.sum(jnp.exp(scores - row_max), axis=-1, keepdims=True))
    softmax_w = jnp.exp(scores - log_total).astype(BF)
    mixed = jnp.einsum("ihqk,ikhd->iqhd", softmax_w, values_all, preferred_element_type=F32)
    return mixed, log_total


def attend_backward(queries, keys_all, values_all, usable, log_total, mixed_grad):
    factor = HEAD_DIM ** (-0.5)
    scores = score_block(queries, keys_all, usable)
    softmax_w = jnp.exp(scores - log_total)
    softmax_low = softmax_w.astype(BF)
    prob_grad = jnp.einsum("iqhd,ikhd->ihqk", mixed_grad, values_all, preferred_element_type=F32)
    inner = jnp.sum(softmax_w * prob_grad, axis=-1, keepdims=True)
    score_grad = (softmax_w * (prob_grad - inner)).astype(BF)
    query_grad = factor * jnp.einsum(
        "ihqk,ikhd->iqhd", score_grad, keys_all, preferred_element_type=F32
    )
    key_grad = factor * jnp.einsum(
        "ihqk,iqhd->ikhd", score_grad, queries, preferred_element_type=F32
    )
    value_grad = jnp.einsum("ihqk,iqhd->ikhd", softmax_low, mixed_grad, preferred_element_type=F32)
    return query_grad, key_grad, value_grad


def matmul(left, right):
    return jnp.einsum("itd,de->ite", left, right, preferred_element_type=F32)


def matmul_back(left, right):
    return jnp.einsum("ite,de->itd", left, right, preferred_element_type=F32)


def outer_sum(left, right):
    return jnp.einsum("itd,ite->de", left, right, preferred_element_type=F32)


def swap_core(value):
    return lax.ppermute(value, "core", [(0, 1), (1, 0)])


def swap_seq(value):
    return lax.ppermute(value, "xl", [(0, 1), (1, 0)])


def swap_x(value, pairs):
    return lax.ppermute(value, RING_X, [p for a, b in pairs for p in ((a, b), (b, a))])


def in_order(index, mine, other, axis):
    first = jnp.where(index == 0, mine, other)
    second = jnp.where(index == 0, other, mine)
    return jnp.stack((first, second), axis=axis)


def join(index, mine, other, axis):
    first = jnp.where(index == 0, mine, other)
    second = jnp.where(index == 0, other, mine)
    return jnp.concatenate((first, second), axis=axis)


def pick(value, index, axis):
    return jnp.where(
        index == 0, lax.index_in_dim(value, 0, axis, False), lax.index_in_dim(value, 1, axis, False)
    )


def gather_chips(block, xh, text_cols=None):
    other = swap_x(block, ((0, 3), (1, 2)))
    if text_cols is not None:
        lo, hi = text_cols
        far = swap_x(block[:, lo:hi], ((0, 2), (1, 3)))
        other = jnp.concatenate((other[:, :lo], far, other[:, hi:]), axis=1)
    pair = in_order(xh, block, other, 0)
    full = lax.all_gather(pair, ("z", "y"), axis=0, tiled=False)
    cols = block.shape[-1]
    full = full.reshape(4, 4, 2, 32, cols)
    return full.transpose(0, 2, 1, 3, 4).reshape(CHIPS * 32, cols)


def scatter_chips(full, xh, text_cols=None):
    cols = full.shape[-1]
    blocks = full.reshape(4, 2, 4, 32, cols).transpose(0, 2, 1, 3, 4).reshape(16 * 64, cols)
    part = lax.psum_scatter(blocks, ("z", "y"), scatter_dimension=0, tiled=True)
    part = part.reshape(2, 32, cols)
    own = pick(part, xh, 0)
    far = pick(part, 1 - xh, 0)
    a = swap_x(own, ((0, 1), (2, 3)))
    b = swap_x(far, ((0, 3), (1, 2)))
    e = swap_x(far, ((0, 2), (1, 3)))
    near = a.astype(F32) + b.astype(F32)
    if text_cols is not None:
        col = lax.broadcasted_iota(jnp.int32, near.shape, 1)
        row = lax.broadcasted_iota(jnp.int32, near.shape, 0)
        is_text = (col >= text_cols[0]) & (col < text_cols[1]) & (row % 16 < 12)
        near = jnp.where(is_text, 0.0, near)
    return (own.astype(F32) + e.astype(F32)) + near


def halves_as_rows(value):
    k = value.shape[-1] // 2
    return jnp.concatenate((value[:, :k], value[:, k:]), axis=0)


def rows_as_halves(value):
    r = value.shape[0] // 2
    return jnp.concatenate((value[:r], value[r:]), axis=1)


def per_device(
    tokens_in,
    noise_emb,
    text_emb,
    prompt_len,
    mod_weight,
    qkv_weight,
    proj_weight,
    cq_weight,
    text_weight,
    co_weight,
    norm_gains,
    up_weight,
    down_weight,
    out_grad,
):
    core = lax.axis_index("core")
    xh = lax.axis_index("xh")
    xl = lax.axis_index("xl")
    rows = tokens_in.shape[1]

    misc = jnp.concatenate(
        (
            noise_emb,
            jnp.pad(text_emb[0], ((0, 0), (0, D - TEXT_W))),
            jnp.broadcast_to(prompt_len.astype(BF)[:, None], (7, D)),
        ),
        axis=0,
    )
    mine = jnp.concatenate((tokens_in[0], out_grad[0], misc), axis=0)
    both = in_order(core, mine, swap_core(mine), 0)
    tokens = both[:, :rows].astype(F32)
    grad_low = both[:, rows : 2 * rows]
    noise = both[:, 2 * rows]
    text = both[:, 2 * rows + 1 : 2 * rows + 9, :TEXT_W]
    lens = both[:, 2 * rows + 9, 0].astype(jnp.int32)

    def side(which):
        up = pick(up_weight.reshape(16, 32, 2, 64), which, 2).reshape(16, C_UP)
        qkv = pick(qkv_weight.reshape(16, 3, 2, 512), which, 2).reshape(16, C_QKV)
        mod = pick(mod_weight.reshape(16, 2, 2, 512), which, 2).reshape(16, C_MOD)
        cq = pick(cq_weight.reshape(16, 2, 512), which, 1)
        txt = pick(text_weight.reshape(12, 2, 2, 256), which, 2).reshape(12, C_TEXT)
        gains = jnp.pad(norm_gains, ((0, 2), (0, C_TEXT - 16)))
        return jnp.concatenate((mod, qkv, cq, jnp.concatenate((txt, gains), axis=0), up), axis=1)

    shared = join(core, side(core), swap_core(side(1 - core)), 0)
    first = jnp.concatenate(
        (
            shared[:, : C_MOD + C_QKV + C_CQ + C_TEXT],
            halves_as_rows(proj_weight),
            halves_as_rows(co_weight),
        ),
        axis=1,
    )
    second = jnp.concatenate(
        (shared[:, C_MOD + C_QKV + C_CQ + C_TEXT :],
         jnp.concatenate((down_weight[:32], down_weight[32:]), axis=1)),
        axis=1,
    )
    full_one = gather_chips(first, xh, TEXT_COLS)
    full_two = gather_chips(second, xh)

    at = 0
    pieces = []
    for width in (C_MOD, C_QKV, C_CQ, C_TEXT, C_PROJ, C_CO):
        pieces.append(full_one[:, at : at + width])
        at += width
    mod_w, qkv_w, cq_w, text_rows, proj_raw, co_raw = pieces
    text_rows = text_rows.reshape(64, 16, C_TEXT)
    text_w = text_rows[:, :12].reshape(TEXT_W, 2, 256)
    gains = text_rows[:, 12:14, :16].transpose(1, 0, 2).reshape(2, D).astype(F32)
    gain_two, gain_three = gains[0], gains[1]
    raw = jnp.stack((proj_raw, co_raw), axis=0).reshape(2, CHIPS, 2, 16, 512)
    raw = raw.transpose(0, 1, 3, 2, 4).reshape(2, 2, 16, 16, D)
    kept = pick(raw, core, 1)
    came = swap_core(pick(raw, 1 - core, 1))
    by_head = in_order(core, kept, came, 2).reshape(2, 512, D)
    proj_w, co_w = by_head[0], by_head[1]
    up_w = full_two[:, :C_UP]
    down_w = full_two[:, C_UP:].reshape(CHIPS, 32, 2, D).transpose(0, 2, 1, 3).reshape(2048, D)

    mod_part = jnp.dot(noise, mod_w, preferred_element_type=F32).reshape(2, 2, 512)
    mod_all = join(core, mod_part, swap_core(mod_part), 2)
    mod_scale, mod_shift = mod_all[:, 0], mod_all[:, 1]
    normed_one = modulated_norm(tokens, mod_scale, mod_shift).astype(BF)
    qkv = matmul(normed_one, qkv_w).astype(BF)
    queries = split_heads(qkv[:, :, :512])
    kv_own = qkv[:, :, 512:]
    kv_all = jnp.concatenate((kv_own, swap_seq(kv_own)), axis=1)
    keys_all = split_heads(kv_all[:, :, :512])
    values_all = split_heads(kv_all[:, :, 512:])
    mixed, self_lse = attend_forward(queries, keys_all, values_all, None)
    attended = mixed.reshape(2, rows, 512).astype(BF)
    proj_part = matmul(attended, proj_w)
    after_self = tokens + (proj_part + swap_core(proj_part))
    normed_two = gained_norm(after_self, gain_two).astype(BF)
    cross_q = split_heads(matmul(normed_two, cq_w).astype(BF))
    text_own = jnp.einsum("ijt,tcn->ijcn", text, text_w, preferred_element_type=F32).astype(BF)
    text_xl = in_order(xl, text_own, swap_seq(text_own), 0)
    text_kv = join(core, pick(text_xl, core, 0), swap_core(pick(text_xl, 1 - core, 0)), 3)
    text_keys = split_heads(text_kv[:, :, 0])
    text_vals = split_heads(text_kv[:, :, 1])
    usable = jnp.arange(TXT, dtype=jnp.int32)[None, :] < lens[:, None]
    cross_heads, cross_lse = attend_forward(cross_q, text_keys, text_vals, usable)
    cross_att = cross_heads.reshape(2, rows, 512).astype(BF)
    co_part = matmul(cross_att, co_w)
    after_cross = after_self + (co_part + swap_core(co_part))
    normed_three = gained_norm(after_cross, gain_three).astype(BF)
    pre_act = matmul(normed_three, up_w)
    activated = jax.nn.gelu(pre_act, approximate=True).astype(BF)
    down_part = matmul(activated, down_w)
    down_own = pick(down_part, core, 0) + swap_core(pick(down_part, 1 - core, 0))
    block_out = (pick(after_cross, core, 0) + down_own).astype(BF)[None]

    down_wg = outer_sum(activated, grad_low)
    act_grad = matmul_back(grad_low, down_w)
    _, gelu_back = jax.vjp(partial(jax.nn.gelu, approximate=True), pre_act)
    pre_grad = gelu_back(act_grad)[0].astype(BF)
    up_wg = outer_sum(normed_three, pre_grad)
    three_part = matmul_back(pre_grad, up_w)
    down_pack = down_wg.reshape(CHIPS, 2, 32, D).transpose(0, 2, 1, 3).reshape(D, C_DOWN)
    grads_two = scatter_chips(
        jnp.concatenate((up_wg.astype(BF), down_pack.astype(BF)), axis=1), xh
    )
    three_grad = three_part + swap_core(three_part)
    _, back_three = jax.vjp(gained_norm, after_cross, gain_three)
    cross_tok_grad, gain_three_grad = back_three(three_grad)
    cross_res_grad = grad_low.astype(F32) + cross_tok_grad
    cross_out_grad = cross_res_grad.astype(BF)
    co_wg = outer_sum(cross_att, cross_out_grad)
    cross_att_grad = matmul_back(cross_out_grad, co_w).astype(BF)
    cq_heads_grad, text_key_grad, text_val_grad = attend_backward(
        cross_q, text_keys, text_vals, usable, cross_lse, split_heads(cross_att_grad)
    )
    text_sum = jnp.stack(
        (text_key_grad.reshape(2, TXT, 512), text_val_grad.reshape(2, TXT, 512)), axis=2
    )
    text_sum = (text_sum + swap_seq(text_sum.astype(BF)).astype(F32)).astype(BF)
    text_quarters = text_sum.reshape(2, TXT, 2, 2, 256)
    text_kept = pick(text_quarters, core, 3)
    text_came = swap_core(pick(text_quarters, 1 - core, 3))
    text_kv_grad = jnp.where(core == xl, text_kept, text_came)
    text_wg = jnp.einsum("ijt,ijcn->tcn", text, text_kv_grad, preferred_element_type=F32)
    text_part = jnp.einsum("ijcn,tcn->ijt", text_kv_grad, text_w, preferred_element_type=F32)
    cross_q_grad = cq_heads_grad.reshape(2, rows, 512).astype(BF)
    cq_wg = outer_sum(normed_two, cross_q_grad)
    two_part = matmul_back(cross_q_grad, cq_w)
    two_grad = two_part + swap_core(two_part)
    _, back_two = jax.vjp(gained_norm, after_self, gain_two)
    self_tok_grad, gain_two_grad = back_two(two_grad)
    self_res_grad = cross_res_grad + self_tok_grad
    proj_out_grad = self_res_grad.astype(BF)
    proj_wg = outer_sum(attended, proj_out_grad)
    attended_grad = matmul_back(proj_out_grad, proj_w).astype(BF)
    query_grad, key_grad, value_grad = attend_backward(
        queries, keys_all, values_all, None, self_lse, split_heads(attended_grad)
    )
    kv_sum = jnp.concatenate(
        (key_grad.reshape(2, 2 * rows, 512), value_grad.reshape(2, 2 * rows, 512)), axis=2
    )
    kv_came = swap_seq(kv_sum[:, rows:].astype(BF))
    kv_grad = (kv_sum[:, :rows] + kv_came.astype(F32)).astype(BF)
    qkv_grad = jnp.concatenate((query_grad.reshape(2, rows, 512).astype(BF), kv_grad), axis=2)
    qkv_wg = outer_sum(normed_one, qkv_grad)
    one_part = matmul_back(qkv_grad, qkv_w)
    one_grad = pick(one_part, core, 0) + swap_core(pick(one_part, 1 - core, 0))

    own_tokens = tokens_in.astype(F32)
    _, mod_back = jax.vjp(
        modulated_norm, own_tokens, pick(mod_scale, core, 0)[None], pick(mod_shift, core, 0)[None]
    )
    input_part, scale_grad, shift_grad = mod_back(one_grad[None])
    tokens_grad = pick(self_res_grad, core, 0)[None] + input_part
    mod_own = jnp.concatenate((scale_grad, shift_grad), axis=0)
    mod_grad = in_order(core, mod_own, swap_core(mod_own), 0)
    mod_half = pick(mod_grad.reshape(2, 2, 2, 512), core, 2).reshape(2, C_MOD)
    mod_wg = jnp.dot(noise.astype(F32).T, mod_half, precision=HIGHEST_PREC)
    noise_part = jnp.dot(mod_half, mod_w.astype(F32).T, precision=HIGHEST_PREC)

    rows_wg = jnp.stack((proj_wg.astype(BF), co_wg.astype(BF)), axis=0).reshape(2, 16, 2, 16, D)
    rows_kept = pick(rows_wg, core, 2)
    rows_came = swap_core(pick(rows_wg, 1 - core, 2))
    rows_all = join(core, rows_kept, rows_came, 1)
    rows_all = rows_all.reshape(2, CHIPS, 16, 2, 512).transpose(0, 1, 3, 2, 4).reshape(2, D, 512)
    gains_wg = jnp.stack((gain_two_grad, gain_three_grad), axis=0).astype(BF)
    gains_wg = jnp.pad(
        gains_wg.reshape(2, 64, 16).transpose(1, 0, 2), ((0, 0), (0, 2), (0, C_TEXT - 16))
    )
    text_pack = jnp.concatenate((text_wg.astype(BF).reshape(64, 12, C_TEXT), gains_wg), axis=1)
    grads_one = scatter_chips(
        jnp.concatenate(
            (
                mod_wg.astype(BF),
                qkv_wg.astype(BF),
                cq_wg.astype(BF),
                text_pack.reshape(D, C_TEXT),
                rows_all[0],
                rows_all[1],
            ),
            axis=1,
        ),
        xh,
        TEXT_COLS,
    )

    shared_cols = C_MOD + C_QKV + C_CQ + C_TEXT
    grads = jnp.concatenate((grads_one[:, :shared_cols], grads_two[:, :C_UP]), axis=1)
    grads = grads.reshape(2, 16, shared_cols + C_UP)
    got = swap_core(pick(grads, 1 - core, 0).astype(BF)).astype(F32)
    kept_cols = pick(grads, core, 0)
    by_core = in_order(core, kept_cols, got, 0)
    at = 0
    pieces = []
    for width in (C_MOD, C_QKV, C_CQ, C_TEXT, C_UP):
        pieces.append(by_core[:, :, at : at + width])
        at += width
    mod_g, qkv_g, cq_g, text_g, up_g = pieces
    mod_wgrad = mod_g.reshape(2, 16, 2, 512).transpose(1, 2, 0, 3).reshape(16, 2 * D)
    qkv_wgrad = qkv_g.reshape(2, 16, 3, 512).transpose(1, 2, 0, 3).reshape(16, 3, D)
    cq_wgrad = cq_g.transpose(1, 0, 2).reshape(16, D)
    text_wgrad = text_g[:, :12].reshape(2, 12, 2, 256).transpose(1, 2, 0, 3).reshape(12, 2, 512)
    gains_grad = kept_cols[12:14, C_MOD + C_QKV + C_CQ : C_MOD + C_QKV + C_CQ + 16]
    up_wgrad = up_g.reshape(2, 16, 32, 64).transpose(1, 2, 0, 3).reshape(16, FF)
    proj_wgrad = rows_as_halves(grads_one[:, shared_cols : shared_cols + C_PROJ])
    co_wgrad = rows_as_halves(grads_one[:, shared_cols + C_PROJ :])
    down_g = grads_two[:, C_UP:]
    down_wgrad = jnp.concatenate((down_g[:, :D], down_g[:, D:]), axis=0)

    small = jnp.concatenate((noise_part[:, None], jnp.pad(text_part, ((0, 0), (0, 0), (0, D - TEXT_W)))), axis=1)
    small = pick(small, core, 0) + swap_core(pick(small, 1 - core, 0))
    small = small + swap_seq(small)
    return (
        block_out,
        tokens_grad,
        small[:1],
        small[None, 1:, :TEXT_W],
        mod_wgrad,
        qkv_wgrad,
        proj_wgrad,
        cq_wgrad,
        text_wgrad,
        co_wgrad,
        gains_grad,
        up_wgrad,
        down_wgrad,
    )


def solution(mesh):
    split = Mesh(mesh.devices.reshape(SIZES), AXES)
    in_specs = (
        P(FSDP, "xl", None),
        P(FSDP, None),
        P(FSDP, None, None),
        P(FSDP),
        P(FSDP, None),
        P(FSDP, None, None),
        P(FSDP, None),
        P(FSDP, None),
        P(FSDP, None, "xl"),
        P(FSDP, None),
        P(None, FSDP),
        P(FSDP, None),
        P(FSDP, None),
        P(FSDP, "xl", None),
    )
    out_specs = (
        P(FSDP, "xl", None),
        P(FSDP, "xl", None),
        P(FSDP, None),
        P(FSDP, None, None),
        P(FSDP, None),
        P(FSDP, None, None),
        P(FSDP, None),
        P(FSDP, None),
        P(FSDP, None, "xl"),
        P(FSDP, None),
        P(None, FSDP),
        P(FSDP, None),
        P(FSDP, None),
    )
    return jax.shard_map(
        per_device, mesh=split, in_specs=in_specs, out_specs=out_specs, check_vma=False
    )
```

time: 4190 us -> 498 us (0.12)
  waiting for transfers between devices: 3890 us -> 165 us
  local copies, waits for them, and re-layouts: 32.4 us -> 151 us
  blocking collectives: 95.6 us -> 0 us
    reduce_scatter x9 -> x2, waiting for transfers between devices: 2390 us -> 52.6 us  [scatter_chips(): part = lax.psum_scatter(blocks, ('z', 'y'), scatter_dimension=0, tiled=True)]
    unnamed x24 -> x4, waiting for transfers between devices: 945 us -> 0.07 us
    all_gather x9 -> x2, waiting for transfers between devices: 490 us -> 64.5 us  [gather_chips(): full = lax.all_gather(pair, ('z', 'y'), axis=0, tiled=False)]
    all_gather x2 -> x0, blocking collectives: 95.6 us -> none  [the longest x1 92.2 us: per_device(): lax.all_gather(norm_gains, 'fsdp', axis=1, tiled=True)]
    psum x2 -> x0, waiting for transfers between devices: 62.3 us -> none  [the longest x1 31.5 us: per_device(): lax.psum(noise_part.astype(jnp.bfloat16), 'seq').astype(jnp.float32)]
    reshape x0 -> x24, local copies, waits for them, and re-layouts: none -> 51.4 us  [the longest x2 16.1 us: gather_chips(): full = full.reshape(4, 4, 2, 32, cols)]
    ppermute x0 -> x30, waiting for transfers between devices: none -> 48.2 us  [the longest x9 32.2 us: swap_x(): lax.ppermute(value, RING_X, [p for a, b in pairs for p in ((a, b), (b, a))])]
    dot_general x25 -> x26, matrix products: 95.6 us -> 57.4 us  [the longest x6 16.2 us: matmul(): return jnp.einsum('itd,de->ite', left, right, preferred_element_type=F32)]
  transfers between devices with their start and end apart: 22 -> 34, of which waited for: 19 -> 17; matrix products, arithmetic and copies ran while one was open for 3% -> 42% of each run, Pallas kernels for 0% -> 0%
where the time goes in v1:
time: 498 us; the launch traced here: 488 us
  waiting for transfers between devices  165 us (33%)
  local copies, waits for them, and re-layouts  151 us (30%)
  matrix products  67.6 us (14%)
  other arithmetic  55.1 us (11%)
  starting transfers between devices  32.8 us (7%)
  between operations  16.7 us (3%)
    all_gather x2, waiting for transfers between devices, gather_chips(): full = lax.all_gather(pair, ('z', 'y'), axis=0, tiled=False)  64.5 us
    reduce_scatter x2, waiting for transfers between devices, scatter_chips(): part = lax.psum_scatter(blocks, ('z', 'y'), scatter_dimension=0, tiled=True)  52.6 us
    ppermute x9, waiting for transfers between devices, swap_x(): lax.ppermute(value, RING_X, [p for a, b in pairs for p in ((a, b), (b, a))])  32.2 us
    unnamed x203, local copies, waits for them, and re-layouts  25.1 us
    dot_general x6, matrix products, matmul(): return jnp.einsum('itd,de->ite', left, right, preferred_element_type=F32)  16.2 us
    transpose x2, local copies, waits for them, and re-layouts, scatter_chips(): full.reshape(4, 2, 4, 32, cols).transpose(0, 2, 1, 3, 4)  16.1 us
    reshape x2, local copies, waits for them, and re-layouts, gather_chips(): full = full.reshape(4, 4, 2, 32, cols)  16.1 us
    dot_general x6, matrix products, outer_sum(): return jnp.einsum('itd,ite->de', left, right, preferred_element_type=F32)  15.6 us
  transfers between devices with their start and end apart: 34, of which 17 were waited for; matrix products, arithmetic and copies ran while one was open for 42% of the time, Pallas kernels for 0%

profile of v1, /device:TPU:1, one launch (start us, length us, event | category | flops | bytes accessed | tf_op | source)
XLA Modules:
  0.0 488.4 jit_solution(15737787811883015028)
XLA Ops:
  17.8 7.0 %collective-permute-done.2 = bf16[32,4608]{1,0:T(8,128)(2,1)S(1)} collective-permute-done((bf16[32,4608]{1,0:T(8,128)(2,1)S(1)}, bf16[32,4608]{1,0:T(8,128)(2,1)S(1)}, u32[]{:S(2)}, u32[]{:S(2)}) %collective-permute-start.2) | collective-permute-done | bytes 294944 | tf_op jit(solution)/shard_map/ppermute | solution.py:105
  28.8 5.3 %collective-permute-done.11 = bf16[32,4096]{1,0:T(8,128)(2,1)S(1)} collective-permute-done((bf16[32,4096]{1,0:T(8,128)(2,1)S(1)}, bf16[32,4096]{1,0:T(8,128)(2,1)S(1)}, u32[]{:S(2)}, u32[]{:S(2)}) %collective-permute-start.11) | collective-permute-done | bytes 262176 | tf_op jit(solution)/shard_map/ppermute | solution.py:105
  42.1 62.4 %all-gather.5.cloned.1.call-done = bf16[32,32,4608]{2,1,0:T(8,128)(2,1)} async-done(((bf16[2,32,4608]{2,1,0:T(8,128)(2,1)}), bf16[32,32,4608]{2,1,0:T(8,128)(2,1)}) %all-gather.5.cloned.1.call-update) | async-done | bytes 9437200 | tf_op jit(solution)/shard_map/all_gather | solution.py:133
  104.5 8.4 %copy.563 = bf16[4,4,2,32,4608]{4,3,1,2,0:T(8,128)(2,1)} copy(bf16[4,4,2,32,4608]{4,3,2,1,0:T(8,128)(2,1)} %bitcast.387) | data formatting | bytes 18874368 | tf_op jit(solution)/shard_map/reshape | solution.py:135
  131.8 4.4 maximum_bitcast_fusion
  177.8 7.7 %copy.582 = bf16[4,4,2,32,4096]{4,3,1,2,0:T(8,128)(2,1)} copy(bf16[4,4,2,32,4096]{4,3,2,1,0:T(8,128)(2,1)} %bitcast.394) | data formatting | bytes 16777216 | tf_op jit(solution)/shard_map/reshape | solution.py:135
  185.5 4.7 slice.484
  190.2 8.2 %reshape.621 = bf16[32,32,2,1024]{3,2,1,0:T(2,128)(2,1)} reshape(bf16[1024,2048]{1,0:T(8,128)(2,1)} %slice.484) | data formatting | bytes 8388608 | tf_op jit(solution)/shard_map/reshape | solution.py:248
  198.4 5.5 %copy.583 = bf16[32,2,32,1024]{3,2,1,0:T(8,128)(2,1)} copy(bf16[32,2,32,1024]{3,1,2,0:T(2,128)(2,1)} %bitcast.382) | data formatting | bytes 8388608 | tf_op jit(solution)/shard_map/transpose | solution.py:248
  206.2 3.6 fusion.1
  209.8 3.7 bitcast_convert_fusion
  216.0 9.0 %copy.611 = bf16[32,2,32,1024]{3,1,2,0:T(2,128)(2,1)} copy(bf16[32,2,32,1024]{3,2,1,0:T(8,128)(2,1)} %bitcast.407) | data formatting | bytes 8388608 | tf_op jit(solution)/shard_map/convert_element_type | solution.py:291
  225.0 5.8 %copy.660 = bf16[128,8,2,1024]{3,1,2,0:T(8,128)(2,1)} copy(bf16[128,8,2,1024]{3,2,1,0:T(2,128)(2,1)} %bitcast.383) | data formatting | bytes 8388608
  234.2 7.9 %pad_maximum_fusion = bf16[1024,4096]{1,0:T(8,128)(2,1)} fusion(bf16[1024,2048]{1,0:T(8,128)(2,1)} %bitcast.384, bf16[1024,2048]{1,0:T(8,128)(2,1)} %bitcast_convert_fusion.1), kind=kLoop, calls=%fused_computation | loop fusion | flops 16777216 | bytes 16777216 | tf_op jit(solution)/shard_map/concatenate | solution.py:291
  242.1 7.8 %copy.612 = bf16[4,4,2,32,4096]{4,3,2,1,0:T(8,128)(2,1)} copy(bf16[4,4,2,32,4096]{4,3,1,2,0:T(8,128)(2,1)} %bitcast.378) | data formatting | bytes 16777216 | tf_op jit(solution)/shard_map/transpose | solution.py:141
  250.0 4.9 fusion
  286.0 3.4 reshape.628
  318.1 7.7 %collective-permute-done.15 = bf16[2,128,1024]{2,1,0:T(8,128)(2,1)} collective-permute-done((bf16[2,128,1024]{2,1,0:T(8,128)(2,1)}, bf16[2,128,1024]{2,1,0:T(8,128)(2,1)}, u32[]{:S(2)}, u32[]{:S(2)}) %collective-permute-start.15) | collective-permute-done | bytes 524320 | tf_op jit(solution)/shard_map/ppermute | solution.py:101
  339.8 4.5 reshape.629
  361.4 8.3 %copy.608 = bf16[4,4,2,32,4608]{4,3,2,1,0:T(8,128)(2,1)} copy(bf16[4,4,2,32,4608]{4,3,1,2,0:T(8,128)(2,1)} %bitcast.113) | data formatting | bytes 18874368 | tf_op jit(solution)/shard_map/transpose | solution.py:141
  369.7 4.3 fusion.115
  392.9 8.9 %collective-permute-done.28 = bf16[32,4096]{1,0:T(8,128)(2,1)S(1)} collective-permute-done((bf16[32,4096]{1,0:T(8,128)(2,1)S(1)}, bf16[32,4096]{1,0:T(8,128)(2,1)S(1)}, u32[]{:S(2)}, u32[]{:S(2)}) %collective-permute-start.28) | collective-permute-done | bytes 262176 | tf_op jit(solution)/shard_map/ppermute | solution.py:105
  402.4 52.6 %reduce-scatter.3.cloned.1.call-done = bf16[64,4608]{1,0:T(8,128)(2,1)} async-done(((bf16[1024,4608]{1,0:T(8,128)(2,1)}), bf16[64,4608]{1,0:T(8,128)(2,1)}) %reduce-scatter.3.cloned.1.call-update) | async-done | bytes 589840 | tf_op jit(solution)/shard_map/reduce_scatter | solution.py:142
  460.1 10.7 %collective-permute-done.25 = bf16[32,4608]{1,0:T(8,128)(2,1)S(1)} collective-permute-done((bf16[32,4608]{1,0:T(8,128)(2,1)S(1)}, bf16[32,4608]{1,0:T(8,128)(2,1)S(1)}, u32[]{:S(2)}, u32[]{:S(2)}) %collective-permute-start.25) | collective-permute-done | bytes 294944 | tf_op jit(solution)/shard_map/ppermute | solution.py:105
  (477 shorter events, 215.2 us)
Async XLA Ops:
  7.2 97.3 %all-gather.5.cloned.1.call-start = ((), (), s32[]{:S(2)}) async-start(), calls=%async_computation.4 | async-start | bytes 10027008 | tf_op jit(solution)/shard_map/all_gather | solution.py:133
  14.6 10.2 %collective-permute-start.2 = (bf16[32,4608]{1,0:T(8,128)(2,1)S(1)}, bf16[32,4608]{1,0:T(8,128)(2,1)S(1)}, u32[]{:S(2)}, u32[]{:S(2)}) collective-permute-start(bf16[32,4608]{1,0:T(8,128)(2,1)S(1)} %maximum_maximum_fusion), channel_id=1, source_target_pairs={{0,17},{17,0},{1,16},{16,1},{2,19},{19,2},{3,18},{18,3},{4,21},{21... | collective-permute-start | bytes 884744 | tf_op jit(solution)/shard_map/ppermute | solution.py:105
  17.2 7.6 %collective-permute-start.3 = (bf16[32,512]{1,0:T(8,128)(2,1)S(1)}, bf16[32,512]{1,0:T(8,128)(2,1)S(1)}, u32[]{:S(2)}, u32[]{:S(2)}) collective-permute-start(bf16[32,512]{1,0:T(8,128)(2,1)S(1)} %fusion.73), channel_id=1, source_target_pairs={{0,16},{16,0},{1,17},{17,1},{2,18},{18,2},{3,19},{19,3},{4,20},{20... | collective-permute-start | bytes 98312 | tf_op jit(solution)/shard_map/ppermute | solution.py:105
  25.9 151.9 %all-gather.7.cloned.1.call-start = ((), (), s32[]{:S(2)}) async-start(), calls=%async_computation.5 | async-start | bytes 8912896 | tf_op jit(solution)/shard_map/all_gather | solution.py:133
  26.0 8.1 %collective-permute-start.11 = (bf16[32,4096]{1,0:T(8,128)(2,1)S(1)}, bf16[32,4096]{1,0:T(8,128)(2,1)S(1)}, u32[]{:S(2)}, u32[]{:S(2)}) collective-permute-start(bf16[32,4096]{1,0:T(8,128)(2,1)S(1)} %fusion.61), channel_id=1, source_target_pairs={{0,17},{17,0},{1,16},{16,1},{2,19},{19,2},{3,18},{18,3},{4,21},{21... | collective-permute-start | bytes 786440 | tf_op jit(solution)/shard_map/ppermute | solution.py:105
  35.0 351.3 %reduce-scatter.5.cloned.1.call-start = ((), (), s32[]{:S(2)}) async-start(), calls=%async_computation.3 | async-start | bytes 8912896 | tf_op jit(solution)/shard_map/reduce_scatter | solution.py:142
  119.6 6.0 %collective-permute-start.4 = (f32[2,2,512]{2,0,1:T(2,128)S(1)}, f32[2,2,512]{2,0,1:T(2,128)S(1)}, u32[]{:S(2)}, u32[]{:S(2)}) collective-permute-start(f32[2,2,512]{2,0,1:T(2,128)S(1)} %fusion.100), channel_id=1, source_target_pairs={{0,2},{2,0},{1,3},{3,1},{4,6},{6,4},{5,7},{7,5},{8,10},{10,8},{9,1... | collective-permute-start | bytes 24584 | tf_op jit(solution)/shard_map/ppermute | solution.py:97
  130.4 14.1 %collective-permute-start.5 = (bf16[2,128,1024]{2,1,0:T(8,128)(2,1)}, bf16[2,128,1024]{2,1,0:T(8,128)(2,1)}, u32[]{:S(2)}, u32[]{:S(2)}) collective-permute-start(bf16[2,128,1024]{2,1,0:T(8,128)(2,1)} %slice.459), channel_id=1, source_target_pairs={{0,1},{1,0},{2,3},{3,2},{4,5},{5,4},{6,7},{7,6},{8,9},{9,8},{10,11... | collective-permute-start | bytes 1572872 | tf_op jit(solution)/shard_map/ppermute | solution.py:101
  140.6 10.4 %collective-permute-start.6 = (bf16[2,16,16,1024]{3,2,1,0:T(8,128)(2,1)}, bf16[2,16,16,1024]{3,2,1,0:T(8,128)(2,1)}, u32[]{:S(2)}, u32[]{:S(2)}) collective-permute-start(bf16[2,16,16,1024]{3,2,1,0:T(8,128)(2,1)} %select_bitcast_fusion.3), channel_id=1, source_target_pairs={{0,2},{2,0},{1,3},{3,1},{4,6},{6,4},{5,7},{7,5},{8,10},{10,8},{9,1... | collective-permute-start | bytes 3145736 | tf_op jit(solution)/shard_map/ppermute | solution.py:97
  155.4 8.7 %collective-permute-start.7 = (f32[2,128,1024]{2,1,0:T(8,128)}, f32[2,128,1024]{2,1,0:T(8,128)}, u32[]{:S(2)}, u32[]{:S(2)}) collective-permute-start(f32[2,128,1024]{2,1,0:T(8,128)} %fusion.132), channel_id=1, source_target_pairs={{0,2},{2,0},{1,3},{3,1},{4,6},{6,4},{5,7},{7,5},{8,10},{10,8},{9,1... | collective-permute-start | bytes 3145736 | tf_op jit(solution)/shard_map/ppermute | solution.py:97
  175.3 28.8 %collective-permute-start.10 = (f32[2,128,1024]{2,1,0:T(8,128)}, f32[2,128,1024]{2,1,0:T(8,128)}, u32[]{:S(2)}, u32[]{:S(2)}) collective-permute-start(f32[2,128,1024]{2,1,0:T(8,128)} %fusion.133), channel_id=1, source_target_pairs={{0,2},{2,0},{1,3},{3,1},{4,6},{6,4},{5,7},{7,5},{8,10},{10,8},{9,1... | collective-permute-start | bytes 3145736 | tf_op jit(solution)/shard_map/ppermute | solution.py:97
  250.0 205.0 %reduce-scatter.3.cloned.1.call-start = ((), (), s32[]{:S(2)}) async-start(), calls=%async_computation.2 | async-start | bytes 10027008 | tf_op jit(solution)/shard_map/reduce_scatter | solution.py:142
  271.8 7.8 %collective-permute-start.18 = (bf16[2,8,2,512]{3,1,0,2:T(8,128)(2,1)S(1)}, bf16[2,8,2,512]{3,1,0,2:T(8,128)(2,1)S(1)}, u32[]{:S(2)}, u32[]{:S(2)}) collective-permute-start(bf16[2,8,2,512]{3,1,0,2:T(8,128)(2,1)S(1)} %convert_element_type.253), channel_id=1, source_target_pairs={{0,1},{1,0},{2,3},{3,2},{4,5},{5,4},{6,7},{7,6},{8,9},{9,8},{10,11... | collective-permute-start | bytes 98312 | tf_op jit(solution)/shard_map/ppermute | solution.py:101
  278.9 10.6 %collective-permute-start.14 = (f32[2,128,1024]{2,1,0:T(8,128)}, f32[2,128,1024]{2,1,0:T(8,128)}, u32[]{:S(2)}, u32[]{:S(2)}) collective-permute-start(f32[2,128,1024]{2,1,0:T(8,128)} %fusion.37), channel_id=1, source_target_pairs={{0,2},{2,0},{1,3},{3,1},{4,6},{6,4},{5,7},{7,5},{8,10},{10,8},{9,1... | collective-permute-start | bytes 3145736 | tf_op jit(solution)/shard_map/ppermute | solution.py:97
  312.5 13.3 %collective-permute-start.15 = (bf16[2,128,1024]{2,1,0:T(8,128)(2,1)}, bf16[2,128,1024]{2,1,0:T(8,128)(2,1)}, u32[]{:S(2)}, u32[]{:S(2)}) collective-permute-start(bf16[2,128,1024]{2,1,0:T(8,128)(2,1)} %fusion.35), channel_id=1, source_target_pairs={{0,1},{1,0},{2,3},{3,2},{4,5},{5,4},{6,7},{7,6},{8,9},{9,8},{10,11... | collective-permute-start | bytes 1572872 | tf_op jit(solution)/shard_map/ppermute | solution.py:101
  317.4 20.4 %collective-permute-start.22 = (bf16[2,16,16,1024]{3,2,1,0:T(8,128)(2,1)S(1)}, bf16[2,16,16,1024]{3,2,1,0:T(8,128)(2,1)S(1)}, u32[]{:S(2)}, u32[]{:S(2)}) collective-permute-start(bf16[2,16,16,1024]{3,2,1,0:T(8,128)(2,1)S(1)} %select_bitcast_fusion), channel_id=1, source_target_pairs={{0,2},{2,0},{1,3},{3,1},{4,6},{6,4},{5,7},{7,5},{8,10},{10,8},{9,1... | collective-permute-start | bytes 3145736 | tf_op jit(solution)/shard_map/ppermute | solution.py:97
  336.7 12.9 %collective-permute-start.17 = (f32[2,1024]{1,0:T(2,128)S(1)}, f32[2,1024]{1,0:T(2,128)S(1)}, u32[]{:S(2)}, u32[]{:S(2)}) collective-permute-start(f32[2,1024]{1,0:T(2,128)S(1)} %pad_maximum_fusion.22), channel_id=1, source_target_pairs={{0,2},{2,0},{1,3},{3,1},{4,6},{6,4},{5,7},{7,5},{8,10},{10,8},{9,1... | collective-permute-start | bytes 24584 | tf_op jit(solution)/shard_map/ppermute | solution.py:97
  385.5 6.2 %collective-permute-start.21 = (f32[9,1024]{1,0:T(8,128)S(1)}, f32[9,1024]{1,0:T(8,128)S(1)}, u32[]{:S(2)}, u32[]{:S(2)}) collective-permute-start(f32[9,1024]{1,0:T(8,128)S(1)} %bitcast_add_fusion.2), channel_id=1, source_target_pairs={{0,1},{1,0},{2,3},{3,2},{4,5},{5,4},{6,7},{7,6},{8,9},{9,8},{10,11... | collective-permute-start | bytes 110600 | tf_op jit(solution)/shard_map/ppermute | solution.py:101
  387.4 14.5 %collective-permute-start.28 = (bf16[32,4096]{1,0:T(8,128)(2,1)S(1)}, bf16[32,4096]{1,0:T(8,128)(2,1)S(1)}, u32[]{:S(2)}, u32[]{:S(2)}) collective-permute-start(bf16[32,4096]{1,0:T(8,128)(2,1)S(1)} %get-tuple-element.137), channel_id=1, source_target_pairs={{0,17},{17,0},{1,16},{16,1},{2,19},{19,2},{3,18},{18,3},{4,21},{21... | collective-permute-start | bytes 786440 | tf_op jit(solution)/shard_map/ppermute | solution.py:105
  389.4 12.8 %collective-permute-start.26 = (bf16[32,4096]{1,0:T(8,128)(2,1)S(1)}, bf16[32,4096]{1,0:T(8,128)(2,1)S(1)}, u32[]{:S(2)}, u32[]{:S(2)}) collective-permute-start(bf16[32,4096]{1,0:T(8,128)(2,1)S(1)} %get-tuple-element.137), channel_id=1, source_target_pairs={{0,16},{16,0},{1,17},{17,1},{2,18},{18,2},{3,19},{19,3},{4,20},{20... | collective-permute-start | bytes 786440 | tf_op jit(solution)/shard_map/ppermute | solution.py:105
  390.0 12.2 %collective-permute-start.27 = (bf16[32,4096]{1,0:T(8,128)(2,1)S(1)}, bf16[32,4096]{1,0:T(8,128)(2,1)S(1)}, u32[]{:S(2)}, u32[]{:S(2)}) collective-permute-start(bf16[32,4096]{1,0:T(8,128)(2,1)S(1)} %get-tuple-element.136), channel_id=1, source_target_pairs={{0,1},{1,0},{16,17},{17,16},{2,3},{3,2},{18,19},{19,18},{4,5},{5,4... | collective-permute-start | bytes 786440 | tf_op jit(solution)/shard_map/ppermute | solution.py:105
  456.0 14.8 %collective-permute-start.25 = (bf16[32,4608]{1,0:T(8,128)(2,1)S(1)}, bf16[32,4608]{1,0:T(8,128)(2,1)S(1)}, u32[]{:S(2)}, u32[]{:S(2)}) collective-permute-start(bf16[32,4608]{1,0:T(8,128)(2,1)S(1)} %get-tuple-element.131), channel_id=1, source_target_pairs={{0,17},{17,0},{1,16},{16,1},{2,19},{19,2},{3,18},{18,3},{4,21},{21... | collective-permute-start | bytes 884744 | tf_op jit(solution)/shard_map/ppermute | solution.py:105
  458.5 12.4 %collective-permute-start.23 = (bf16[32,4608]{1,0:T(8,128)(2,1)S(1)}, bf16[32,4608]{1,0:T(8,128)(2,1)S(1)}, u32[]{:S(2)}, u32[]{:S(2)}) collective-permute-start(bf16[32,4608]{1,0:T(8,128)(2,1)S(1)} %get-tuple-element.131), channel_id=1, source_target_pairs={{0,16},{16,0},{1,17},{17,1},{2,18},{18,2},{3,19},{19,3},{4,20},{20... | collective-permute-start | bytes 884744 | tf_op jit(solution)/shard_map/ppermute | solution.py:105
  459.1 11.8 %collective-permute-start.24 = (bf16[32,4608]{1,0:T(8,128)(2,1)S(1)}, bf16[32,4608]{1,0:T(8,128)(2,1)S(1)}, u32[]{:S(2)}, u32[]{:S(2)}) collective-permute-start(bf16[32,4608]{1,0:T(8,128)(2,1)S(1)} %get-tuple-element.130), channel_id=1, source_target_pairs={{0,1},{1,0},{16,17},{17,16},{2,3},{3,2},{18,19},{19,18},{4,5},{5,4... | collective-permute-start | bytes 884744 | tf_op jit(solution)/shard_map/ppermute | solution.py:105
  (101 other events, 672.9 us)
Sparse Core Ops, SparseCore 0:
  26.0 78.4 all-gather.4
  107.2 70.5 all-gather.6
  250.1 83.8 reduce-scatter.4
  369.8 85.0 reduce-scatter.2

commit v2 on v1

v2 whole, which is shorter than its diff:
```python
import jax
import jax.numpy as jnp
from jax import lax
from jax.experimental import pallas as pl
from jax.experimental.pallas import tpu as pltpu
from jax.sharding import Mesh
from jax.sharding import PartitionSpec as P

HEAD_DIM = 64
EPSILON = 1e-06
HIGHEST_PREC = lax.Precision.HIGHEST
NEG_LARGE = -1e30
BF = jnp.bfloat16
F32 = jnp.float32

AXES = ("z", "xh", "y", "core", "xl")
SIZES = (4, 2, 4, 2, 2)
FSDP = ("z", "xh", "y", "core")
RING_X = ("xh", "xl")

D = 1024
FF = 4096
TEXT_W = 768
TXT = 8
CHIPS = 32

C_MOD, C_QKV, C_CQ, C_TEXT, C_PROJ, C_CO = 1024, 1536, 512, 512, 512, 512
TEXT_COLS = (C_MOD + C_QKV + C_CQ, C_MOD + C_QKV + C_CQ + C_TEXT)
C_UP, C_DOWN = 2048, 2048


def rms_norm(tensor):
    return tensor * lax.rsqrt(jnp.mean(tensor * tensor, axis=-1, keepdims=True) + EPSILON)


def modulated_norm(tensor, scale, shift):
    return rms_norm(tensor) * (1.0 + scale[:, None, :]) + shift[:, None, :]


def mm(a, b):
    return jnp.dot(a, b, preferred_element_type=F32)


def mm_nt(a, b):
    return lax.dot_general(a, b, (((1,), (1,)), ((), ())), preferred_element_type=F32)


def mm_tn(a, b):
    return lax.dot_general(a, b, (((0,), (0,)), ((), ())), preferred_element_type=F32)


CHIP_ORDER = [(z, xh, y) for z in range(4) for xh in range(2) for y in range(4)]


def nat(ref):
    return jnp.concatenate([ref[z, y, xh] for z, xh, y in CHIP_ORDER], axis=0)


def store_nat(ref, value):
    for i, (z, xh, y) in enumerate(CHIP_ORDER):
        ref[z, y, xh] = value[32 * i : 32 * i + 32].astype(ref.dtype)


def norm_of(x):
    inv = lax.rsqrt(jnp.mean(x * x, axis=-1, keepdims=True) + EPSILON)
    return x * inv, inv


def norm_grad(unit, inv, dh_w):
    return (dh_w - unit * jnp.mean(dh_w * unit, axis=-1, keepdims=True)) * inv


def call(body, outs, ins, scratch=(), specs=None, out_specs=None, grid=None, prefetch=0):
    whole = pl.BlockSpec(memory_space=pltpu.VMEM)
    return pl.pallas_call(
        body,
        out_shape=outs,
        grid_spec=pltpu.PrefetchScalarGridSpec(
            num_scalar_prefetch=prefetch,
            grid=grid or (),
            in_specs=specs or [whole] * len(ins),
            out_specs=out_specs or [whole] * len(outs),
            scratch_shapes=list(scratch),
        ),
        compiler_params=pltpu.CompilerParams(vmem_limit_bytes=60 * 1024 * 1024),
    )(*ins)


def shape(dims, dtype):
    return jax.ShapeDtypeStruct(dims, dtype)


WHOLE = pl.BlockSpec(memory_space=pltpu.VMEM)
SMEM = pl.BlockSpec(memory_space=pltpu.SMEM)


def cols_spec(block, width=512):
    return pl.BlockSpec((4, 4, 2, 32, width), lambda i: (0, 0, 0, 0, block))


def fixed(dims):
    return pl.BlockSpec(dims, lambda i: (0,) * len(dims))


def mod_body(noise, w, out):
    out[...] = mm(noise[...], nat(w))


def mod_kernel(noise, full):
    return call(
        mod_body,
        [shape((2, 1024), F32)],
        (noise, full),
        specs=[fixed((2, D)), cols_spec(0, 1024)],
        out_specs=[fixed((2, 1024))],
        grid=(1,),
    )[0]


def qkv_body(tok, scale, shift, wq, wk, wv, n1_out, q_out, kv_out):
    for b in range(2):
        r = slice(128 * b, 128 * b + 128)
        unit, _ = norm_of(tok[r].astype(F32))
        n1_out[r] = (unit * (1.0 + scale[b : b + 1]) + shift[b : b + 1]).astype(BF)
    n1 = n1_out[...]
    q_out[...] = mm(n1, nat(wq)).astype(BF)
    kv_out[:, :512] = mm(n1, nat(wk)).astype(BF)
    kv_out[:, 512:] = mm(n1, nat(wv)).astype(BF)


def qkv_kernel(tok, scale, shift, full):
    return call(
        qkv_body,
        [shape((256, D), BF), shape((256, 512), BF), shape((256, D), BF)],
        (tok, scale, shift, full, full, full),
        specs=[fixed((256, D)), fixed((2, D)), fixed((2, D)), cols_spec(2), cols_spec(3), cols_spec(4)],
        out_specs=[fixed((256, D)), fixed((256, 512)), fixed((256, D))],
        grid=(1,),
    )


def head_cols(h):
    return slice(64 * h, 64 * h + 64)


def self_probs(q, k):
    scores = mm_nt(q, k) * HEAD_DIM ** (-0.5)
    e = jnp.exp(scores - jnp.max(scores, axis=-1, keepdims=True))
    return e * (1.0 / jnp.sum(e, axis=-1, keepdims=True))


def attend_body(q, kv, kv_far, proj_w, att_out, part_out):
    for b in range(2):
        r = slice(128 * b, 128 * b + 128)
        for h in range(8):
            k = jnp.concatenate((kv[r, head_cols(h)], kv_far[r, head_cols(h)]), axis=0)
            v = jnp.concatenate((kv[r, head_cols(8 + h)], kv_far[r, head_cols(8 + h)]), axis=0)
            p = self_probs(q[r, head_cols(h)], k).astype(BF)
            att_out[r, head_cols(h)] = mm(p, v).astype(BF)
    part_out[...] = mm(att_out[...], proj_w[...])


def attend_kernel(q, kv, kv_far, proj_w):
    return call(
        attend_body, [shape((256, 512), BF), shape((256, D), F32)], (q, kv, kv_far, proj_w)
    )


def spread_heads(rows8):
    tall = jnp.concatenate([rows8.astype(F32)] * 16, axis=0)
    row = lax.broadcasted_iota(jnp.int32, tall.shape, 0) // 8
    col = lax.broadcasted_iota(jnp.int32, tall.shape, 1) // 64
    return jnp.where(row == col, tall, 0.0).astype(BF)


def fold_heads(tall):
    row = lax.broadcasted_iota(jnp.int32, tall.shape, 0) // 8
    col = lax.broadcasted_iota(jnp.int32, tall.shape, 1) // 64
    kept = jnp.where(row == col, tall, 0.0)
    total = kept[0:8]
    for h in range(1, 8):
        total = total + kept[8 * h : 8 * h + 8]
    return total


def by_eights(op, x):
    lane = lax.broadcasted_iota(jnp.int32, x.shape, 1)
    for step in (1, 2, 4):
        up = pltpu.roll(x, x.shape[1] - step, 1)
        down = pltpu.roll(x, step, 1)
        x = op(x, jnp.where((lane & step) == 0, up, down))
    return x


def cross_probs(q, keys, length):
    scores = mm_nt(q, keys) * HEAD_DIM ** (-0.5)
    lane = lax.broadcasted_iota(jnp.int32, scores.shape, 1)
    scores = jnp.where((lane & 7) < length, scores, NEG_LARGE)
    e = jnp.exp(scores - by_eights(jnp.maximum, scores))
    return e * (1.0 / by_eights(jnp.add, e))


def cross_body(
    tok, part, part_far, gains, cq_w, text_kv, lens, co_w, res_out, n2_out, cq_out, att_out, part_out
):
    res_out[...] = tok[...].astype(F32) + (part[...] + part_far[...])
    unit, _ = norm_of(res_out[...])
    n2_out[...] = (unit * gains[0:1]).astype(BF)
    cq_out[...] = mm(n2_out[...], nat(cq_w)).astype(BF)
    for b in range(2):
        r = slice(128 * b, 128 * b + 128)
        keys = spread_heads(text_kv[b, :, 0:512])
        vals = spread_heads(text_kv[b, :, 512:1024])
        p = cross_probs(cq_out[r], keys, lens[b]).astype(BF)
        att_out[r] = mm(p, vals).astype(BF)
    part_out[...] = mm(att_out[...], co_w[...])


def cross_kernel(tok, part, part_far, gains, full, text_kv, lens, co_w):
    f = fixed
    return call(
        cross_body,
        [
            shape((256, D), F32),
            shape((256, D), BF),
            shape((256, 512), BF),
            shape((256, 512), BF),
            shape((256, D), F32),
        ],
        (tok, part, part_far, gains, full, text_kv, lens, co_w),
        specs=[
            f((256, D)),
            f((256, D)),
            f((256, D)),
            f((2, D)),
            cols_spec(5),
            f((2, 8, D)),
            SMEM,
            f((512, D)),
        ],
        out_specs=[f((256, D)), f((256, D)), f((256, 512)), f((256, 512)), f((256, D))],
        grid=(1,),
    )


GELU_A = 0.7978845608028654
GELU_B = 0.044715


def ff_body(
    res, part, part_far, gains, og, up, down, res_out, grad_out, three_out, down_out, n3, g_up, g_down
):
    i = pl.program_id(0)

    @pl.when(i == 0)
    def _():
        res_out[...] = res[...] + (part[...] + part_far[...])
        unit, _ = norm_of(res_out[...])
        n3[...] = (unit * gains[1:2]).astype(BF)

    up_w = nat(up)
    down_w = jnp.concatenate(
        [
            down[0, y, xh, :, D * h : D * h + D]
            for xh in range(2)
            for y in range(4)
            for h in range(2)
        ],
        axis=0,
    )
    pre = mm(n3[...], up_w)
    t = jnp.tanh(GELU_A * (pre + GELU_B * (pre * pre * pre)))
    act = (0.5 * pre * (1.0 + t)).astype(BF)
    slope = 0.5 * (1.0 + t) + 0.5 * pre * (1.0 - t * t) * (
        GELU_A * (1.0 + 3.0 * GELU_B * (pre * pre))
    )
    pre_grad = (mm_nt(og[...], down_w) * slope).astype(BF)
    down_part = mm(act, down_w)
    three_part = mm_nt(pre_grad, up_w)

    @pl.when(i == 0)
    def _():
        down_out[...] = down_part
        three_out[...] = three_part

    @pl.when(i > 0)
    def _():
        down_out[...] += down_part
        three_out[...] += three_part

    up_wg = mm_tn(n3[...], pre_grad).astype(BF)
    down_wg = mm_tn(act, og[...]).astype(BF)
    for j, (z, xh, y) in enumerate(CHIP_ORDER):
        g_up[z, y, xh] = up_wg[32 * j : 32 * j + 32]
    j = 0
    for xh in range(2):
        for y in range(4):
            for h in range(2):
                g_down[0, y, xh, :, D * h : D * h + D] = down_wg[32 * j : 32 * j + 32]
                j += 1
    grad_out[:, :, :, :, pl.ds(pl.multiple_of(i * 512, 512), 512)] = g_up[...]
    grad_out[pl.ds(i, 1), :, :, :, C_UP:] = g_down[...]


def ff_kernel(res, part, part_far, gains, og, full):
    f = fixed
    return call(
        ff_body,
        [
            shape((256, D), F32),
            shape((4, 4, 2, 32, C_UP + C_DOWN), BF),
            shape((256, D), F32),
            shape((256, D), F32),
        ],
        (res, part, part_far, gains, og, full, full),
        scratch=[
            pltpu.VMEM((256, D), BF),
            pltpu.VMEM((4, 4, 2, 32, 512), BF),
            pltpu.VMEM((1, 4, 2, 32, 2048), BF),
        ],
        specs=[
            f((256, D)),
            f((256, D)),
            f((256, D)),
            f((2, D)),
            f((256, D)),
            pl.BlockSpec((4, 4, 2, 32, 512), lambda i: (0, 0, 0, 0, i)),
            pl.BlockSpec((1, 4, 2, 32, 2048), lambda i: (i, 0, 0, 0, 1)),
        ],
        out_specs=[f((256, D)), f((4, 4, 2, 32, C_UP + C_DOWN)), f((256, D)), f((256, D))],
        grid=(4,),
    )


def cross_back_body(
    part, part_far, res, og, gains, att, cq, n2, text_kv, lens, co_w, cq_w,
    grad_out, gain_out, co_out, cqw_out, text_out, two_out, ag, dq,
):
    unit, inv = norm_of(res[...])
    three = part[...] + part_far[...]
    gain_out[...] = jnp.sum(three * unit, axis=0, keepdims=True)
    grad_out[...] = og[...].astype(F32) + norm_grad(unit, inv, three * gains[1:2])
    low = grad_out[...].astype(BF)
    co_out[...] = mm_tn(att[...], low).astype(BF)
    ag[...] = mm_nt(low, co_w[...]).astype(BF)
    for b in range(2):
        r = slice(128 * b, 128 * b + 128)
        keys = spread_heads(text_kv[b, :, 0:512])
        vals = spread_heads(text_kv[b, :, 512:1024])
        p = cross_probs(cq[r], keys, lens[b])
        dp = mm_nt(ag[r], vals)
        ds = (p * (dp - by_eights(jnp.add, p * dp))).astype(BF)
        dq[r] = (mm(ds, keys) * HEAD_DIM ** (-0.5)).astype(BF)
        text_out[b, :, 0:512] = fold_heads(mm_tn(ds, cq[r])) * HEAD_DIM ** (-0.5)
        text_out[b, :, 512:1024] = fold_heads(mm_tn(p.astype(BF), ag[r]))
    store_nat(cqw_out, mm_tn(n2[...], dq[...]))
    two_out[...] = mm_nt(dq[...], nat(cq_w))


def cross_back_kernel(part, part_far, res, og, gains, att, cq, n2, text_kv, lens, co_w, full):
    f = fixed
    return call(
        cross_back_body,
        [
            shape((256, D), F32),
            shape((1, D), F32),
            shape((512, D), BF),
            shape((4, 4, 2, 32, 512), BF),
            shape((2, 8, D), F32),
            shape((256, D), F32),
        ],
        (part, part_far, res, og, gains, att, cq, n2, text_kv, lens, co_w, full),
        scratch=[pltpu.VMEM((256, 512), BF), pltpu.VMEM((256, 512), BF)],
        specs=[
            f((256, D)),
            f((256, D)),
            f((256, D)),
            f((256, D)),
            f((2, D)),
            f((256, 512)),
            f((256, 512)),
            f((256, D)),
            f((2, 8, D)),
            SMEM,
            f((512, D)),
            cols_spec(5),
        ],
        out_specs=[
            f((256, D)),
            f((1, D)),
            f((512, D)),
            f((4, 4, 2, 32, 512)),
            f((2, 8, D)),
            f((256, D)),
        ],
        grid=(1,),
    )


def self_back_body(
    part, part_far, res, res_grad, gains, att, q, kv, kv_far, proj_w,
    grad_out, gain_out, proj_out, dq_out, dkv_out, dfar_out, ag,
):
    unit, inv = norm_of(res[...])
    two = part[...] + part_far[...]
    gain_out[...] = jnp.sum(two * unit, axis=0, keepdims=True)
    grad_out[...] = res_grad[...] + norm_grad(unit, inv, two * gains[0:1])
    low = grad_out[...].astype(BF)
    proj_out[...] = mm_tn(att[...], low).astype(BF)
    ag[...] = mm_nt(low, proj_w[...]).astype(BF)
    factor = HEAD_DIM ** (-0.5)
    for b in range(2):
        r = slice(128 * b, 128 * b + 128)
        for h in range(8):
            kc, vc = head_cols(h), head_cols(8 + h)
            k = jnp.concatenate((kv[r, kc], kv_far[r, kc]), axis=0)
            v = jnp.concatenate((kv[r, vc], kv_far[r, vc]), axis=0)
            qh = q[r, kc]
            gh = ag[r, kc]
            p = self_probs(qh, k)
            dp = mm_nt(gh, v)
            ds = (p * (dp - jnp.sum(p * dp, axis=-1, keepdims=True))).astype(BF)
            dq_out[r, kc] = (mm(ds, k) * factor).astype(BF)
            dk = mm_tn(ds, qh) * factor
            dv = mm_tn(p.astype(BF), gh)
            dkv_out[r, kc] = dk[:128]
            dkv_out[r, vc] = dv[:128]
            dfar_out[r, kc] = dk[128:].astype(BF)
            dfar_out[r, vc] = dv[128:].astype(BF)


def self_back_kernel(part, part_far, res, res_grad, gains, att, q, kv, kv_far, proj_w):
    return call(
        self_back_body,
        [
            shape((256, D), F32),
            shape((1, D), F32),
            shape((512, D), BF),
            shape((256, 512), BF),
            shape((256, D), F32),
            shape((256, D), BF),
        ],
        (part, part_far, res, res_grad, gains, att, q, kv, kv_far, proj_w),
        scratch=[pltpu.VMEM((256, 512), BF)],
    )


def qkv_back_body(dq, dkv, dfar, n1, wq, wk, wv, wg_out, part_out):
    n = n1[...]
    dqv = dq[...]
    dkvv = (dkv[...] + dfar[...].astype(F32)).astype(BF)
    grads = (dqv, dkvv[:, :512], dkvv[:, 512:])
    total = None
    for i, (g, w) in enumerate(zip(grads, (wq, wk, wv))):
        wg = mm_tn(n, g).astype(BF)
        for j, (z, xh, y) in enumerate(CHIP_ORDER):
            wg_out[z, y, xh, :, 512 * i : 512 * i + 512] = wg[32 * j : 32 * j + 32]
        t = mm_nt(g, nat(w))
        total = t if total is None else total + t
    part_out[...] = total


def qkv_back_kernel(dq, dkv, dfar, n1, full):
    f = fixed
    return call(
        qkv_back_body,
        [shape((4, 4, 2, 32, 1536), BF), shape((256, D), F32)],
        (dq, dkv, dfar, n1, full, full, full),
        specs=[
            f((256, 512)),
            f((256, D)),
            f((256, D)),
            f((256, D)),
            cols_spec(2),
            cols_spec(3),
            cols_spec(4),
        ],
        out_specs=[f((4, 4, 2, 32, 1536)), f((256, D))],
        grid=(1,),
    )


def rows_body(core, kept, came, proj_out, co_out):
    first = core[0] == 0
    i = 0
    for z in range(2):
        for xh in range(2):
            for y in range(4):
                a, b = kept[z, y, xh], came[z, y, xh]
                for bit in range(2):
                    t = jnp.where(first, a, b) if bit == 0 else jnp.where(first, b, a)
                    for out, c in ((proj_out, 0), (co_out, 512)):
                        out[16 * i : 16 * i + 16, :512] = t[:16, c : c + 512]
                        out[16 * i : 16 * i + 16, 512:] = t[16:, c : c + 512]
                    i += 1


def rows_kernel(core, kept, came):
    return call(
        rows_body,
        [shape((512, D), BF), shape((512, D), BF)],
        (core, kept, came),
        specs=[SMEM, WHOLE, WHOLE],
    )


def rows_back_body(core, proj_wg, co_wg, kept_out, sent_out):
    first = core[0] == 0
    i = 0
    for z in range(2):
        for xh in range(2):
            for y in range(4):
                t = []
                for bit in range(2):
                    r = slice(16 * i, 16 * i + 16)
                    t.append(
                        jnp.concatenate(
                            (
                                jnp.concatenate((proj_wg[r, :512], proj_wg[r, 512:]), axis=0),
                                jnp.concatenate((co_wg[r, :512], co_wg[r, 512:]), axis=0),
                            ),
                            axis=1,
                        )
                    )
                    i += 1
                kept_out[z, y, xh] = jnp.where(first, t[0], t[1])
                sent_out[z, y, xh] = jnp.where(first, t[1], t[0])


def rows_back_kernel(core, proj_wg, co_wg):
    dims = shape((2, 4, 2, 32, D), BF)
    return call(
        rows_back_body, [dims, dims], (core, proj_wg, co_wg), specs=[SMEM, WHOLE, WHOLE]
    )


def swap_core(value):
    return lax.ppermute(value, "core", [(0, 1), (1, 0)])


def swap_seq(value):
    return lax.ppermute(value, "xl", [(0, 1), (1, 0)])


def swap_x(value, pairs):
    return lax.ppermute(value, RING_X, [p for a, b in pairs for p in ((a, b), (b, a))])


def in_order(index, mine, other, axis):
    first = jnp.where(index == 0, mine, other)
    second = jnp.where(index == 0, other, mine)
    return jnp.stack((first, second), axis=axis)


def join(index, mine, other, axis):
    first = jnp.where(index == 0, mine, other)
    second = jnp.where(index == 0, other, mine)
    return jnp.concatenate((first, second), axis=axis)


def pick(value, index, axis):
    return jnp.where(
        index == 0, lax.index_in_dim(value, 0, axis, False), lax.index_in_dim(value, 1, axis, False)
    )


def gather_chips(block, xh, text_cols=None):
    other = swap_x(block, ((0, 3), (1, 2)))
    if text_cols is not None:
        lo, hi = text_cols
        far = swap_x(block[:, lo:hi], ((0, 2), (1, 3)))
        other = jnp.concatenate((other[:, :lo], far, other[:, hi:]), axis=1)
    pair = in_order(xh, block, other, 0)
    full = lax.all_gather(pair, ("z", "y"), axis=0, tiled=False)
    cols = block.shape[-1]
    return full.reshape(4, 4, 2, 32, cols)


def scatter_chips(full, xh, text_cols=None):
    cols = full.shape[-1]
    part = lax.psum_scatter(full.reshape(D, cols), ("z", "y"), scatter_dimension=0, tiled=True)
    part = part.reshape(2, 32, cols)
    own = pick(part, xh, 0)
    far = pick(part, 1 - xh, 0)
    a = swap_x(own, ((0, 1), (2, 3)))
    b = swap_x(far, ((0, 3), (1, 2)))
    e = swap_x(far, ((0, 2), (1, 3)))
    near = a.astype(F32) + b.astype(F32)
    if text_cols is not None:
        col = lax.broadcasted_iota(jnp.int32, near.shape, 1)
        row = lax.broadcasted_iota(jnp.int32, near.shape, 0)
        is_text = (col >= text_cols[0]) & (col < text_cols[1]) & (row % 16 < 12)
        near = jnp.where(is_text, 0.0, near)
    return (own.astype(F32) + e.astype(F32)) + near


def halves_as_rows(value):
    k = value.shape[-1] // 2
    return jnp.concatenate((value[:, :k], value[:, k:]), axis=0)


def rows_as_halves(value):
    r = value.shape[0] // 2
    return jnp.concatenate((value[:r], value[r:]), axis=1)


def per_device(
    tokens_in,
    noise_emb,
    text_emb,
    prompt_len,
    mod_weight,
    qkv_weight,
    proj_weight,
    cq_weight,
    text_weight,
    co_weight,
    norm_gains,
    up_weight,
    down_weight,
    out_grad,
):
    core = lax.axis_index("core")
    xh = lax.axis_index("xh")
    xl = lax.axis_index("xl")
    rows = tokens_in.shape[1]

    misc = jnp.concatenate(
        (
            noise_emb,
            jnp.pad(text_emb[0], ((0, 0), (0, D - TEXT_W))),
            jnp.broadcast_to(prompt_len.astype(BF)[:, None], (7, D)),
        ),
        axis=0,
    )
    mine = jnp.concatenate((tokens_in[0], out_grad[0], misc), axis=0)
    both = in_order(core, mine, swap_core(mine), 0)
    tok = both[:, :rows].reshape(256, D)
    og = both[:, rows : 2 * rows].reshape(256, D)
    noise = both[:, 2 * rows]
    text = both[:, 2 * rows + 1 : 2 * rows + 9, :TEXT_W]
    lens = both[:, 2 * rows + 9, 0].astype(jnp.int32)

    def side(which):
        up = pick(up_weight.reshape(16, 32, 2, 64), which, 2).reshape(16, C_UP)
        qkv = pick(qkv_weight.reshape(16, 3, 2, 512), which, 2).reshape(16, C_QKV)
        mod = pick(mod_weight.reshape(16, 2, 2, 512), which, 2).reshape(16, C_MOD)
        cq = pick(cq_weight.reshape(16, 2, 512), which, 1)
        txt = pick(text_weight.reshape(12, 2, 2, 256), which, 2).reshape(12, C_TEXT)
        gains = jnp.pad(norm_gains, ((0, 2), (0, C_TEXT - 16)))
        return jnp.concatenate((mod, qkv, cq, jnp.concatenate((txt, gains), axis=0), up), axis=1)

    shared = join(core, side(core), swap_core(side(1 - core)), 0)
    first = jnp.concatenate(
        (
            shared[:, : C_MOD + C_QKV + C_CQ + C_TEXT],
            halves_as_rows(proj_weight),
            halves_as_rows(co_weight),
        ),
        axis=1,
    )
    second = jnp.concatenate(
        (
            shared[:, C_MOD + C_QKV + C_CQ + C_TEXT :],
            jnp.concatenate((down_weight[:32], down_weight[32:]), axis=1),
        ),
        axis=1,
    )
    full_one = gather_chips(first, xh, TEXT_COLS)
    full_two = gather_chips(second, xh)

    text_rows = full_one[..., TEXT_COLS[0] : TEXT_COLS[1]].transpose(0, 2, 1, 3, 4)
    text_rows = text_rows.reshape(64, 16, C_TEXT)
    text_w = text_rows[:, :12].reshape(TEXT_W, 2, 256)
    gains = text_rows[:, 12:14, :16].transpose(1, 0, 2).reshape(2, D).astype(F32)
    halves = full_one[..., TEXT_COLS[1] :].reshape(2, 2, 4, 2, 32, D)
    kept = pick(halves, core, 0)
    core_id = core.astype(jnp.int32)[None]
    proj_w, co_w = rows_kernel(core_id, kept, swap_core(pick(halves, 1 - core, 0)))

    mod_part = mod_kernel(noise, full_one).reshape(2, 2, 512)
    mod_all = join(core, mod_part, swap_core(mod_part), 2)
    mod_scale, mod_shift = mod_all[:, 0], mod_all[:, 1]
    normed_one, queries, kv_own = qkv_kernel(tok, mod_scale, mod_shift, full_one)
    kv_far = swap_seq(kv_own)
    attended, proj_part = attend_kernel(queries, kv_own, kv_far, proj_w)
    text_own = jnp.einsum("ijt,tcn->ijcn", text, text_w, preferred_element_type=F32).astype(BF)
    text_xl = in_order(xl, text_own, swap_seq(text_own), 0)
    text_kv = join(core, pick(text_xl, core, 0), swap_core(pick(text_xl, 1 - core, 0)), 3)
    text_kv = text_kv.reshape(2, TXT, D)
    after_self, normed_two, cross_q, cross_att, co_part = cross_kernel(
        tok, proj_part, swap_core(proj_part), gains, full_one, text_kv, lens, co_w
    )
    after_cross, grads_ff, three_part, down_part = ff_kernel(
        after_self, co_part, swap_core(co_part), gains, og, full_two
    )
    grads_two = scatter_chips(grads_ff, xh)
    down_part = down_part.reshape(2, rows, D)
    down_own = pick(down_part, core, 0) + swap_core(pick(down_part, 1 - core, 0))
    block_out = (pick(after_cross.reshape(2, rows, D), core, 0) + down_own).astype(BF)[None]

    cross_res_grad, gain_three_grad, co_wg, cq_wg, text_sum, two_part = cross_back_kernel(
        three_part, swap_core(three_part), after_cross, og, gains, cross_att, cross_q,
        normed_two, text_kv, lens, co_w, full_one,
    )
    self_res_grad, gain_two_grad, proj_wg, dq, dkv, dkv_far = self_back_kernel(
        two_part, swap_core(two_part), after_self, cross_res_grad, gains, attended, queries,
        kv_own, kv_far, proj_w,
    )
    qkv_wg, one_part = qkv_back_kernel(dq, dkv, swap_seq(dkv_far), normed_one, full_one)

    text_sum = (text_sum + swap_seq(text_sum.astype(BF)).astype(F32)).astype(BF)
    text_quarters = text_sum.reshape(2, TXT, 2, 2, 256)
    text_kept = pick(text_quarters, core, 3)
    text_came = swap_core(pick(text_quarters, 1 - core, 3))
    text_kv_grad = jnp.where(core == xl, text_kept, text_came)
    text_wg = jnp.einsum("ijt,ijcn->tcn", text, text_kv_grad, preferred_element_type=F32)
    text_part = jnp.einsum("ijcn,tcn->ijt", text_kv_grad, text_w, preferred_element_type=F32)

    one_part = one_part.reshape(2, rows, D)
    one_grad = pick(one_part, core, 0) + swap_core(pick(one_part, 1 - core, 0))
    own_tokens = tokens_in.astype(F32)
    _, mod_back = jax.vjp(
        modulated_norm, own_tokens, pick(mod_scale, core, 0)[None], pick(mod_shift, core, 0)[None]
    )
    input_part, scale_grad, shift_grad = mod_back(one_grad[None])
    tokens_grad = pick(self_res_grad.reshape(2, rows, D), core, 0)[None] + input_part
    mod_own = jnp.concatenate((scale_grad, shift_grad), axis=0)
    mod_grad = in_order(core, mod_own, swap_core(mod_own), 0)
    mod_half = pick(mod_grad.reshape(2, 2, 2, 512), core, 2).reshape(2, C_MOD)
    noise_f = noise.astype(F32)
    noise_rows = noise_f.reshape(2, 4, 2, 4, 32).transpose(0, 1, 3, 2, 4)[..., None]
    mod_wg = noise_rows[0] * mod_half[0] + noise_rows[1] * mod_half[1]
    mod_w = full_one[..., :C_MOD].astype(F32)
    noise_part = jnp.einsum("ic,zyxrc->izxyr", mod_half, mod_w, precision=HIGHEST_PREC)
    noise_part = noise_part.reshape(2, D)

    rows_kept, rows_sent = rows_back_kernel(core_id, proj_wg, co_wg)
    rows_all = join(core, rows_kept, swap_core(rows_sent), 0)
    gains_wg = jnp.concatenate((gain_two_grad, gain_three_grad), axis=0).astype(BF)
    gains_wg = jnp.pad(
        gains_wg.reshape(2, 64, 16).transpose(1, 0, 2), ((0, 0), (0, 2), (0, C_TEXT - 16))
    )
    text_pack = jnp.concatenate((text_wg.astype(BF).reshape(64, 12, C_TEXT), gains_wg), axis=1)
    text_pack = text_pack.reshape(4, 2, 4, 32, C_TEXT).transpose(0, 2, 1, 3, 4)
    grads_one = scatter_chips(
        jnp.concatenate((mod_wg.astype(BF), qkv_wg, cq_wg, text_pack, rows_all), axis=4),
        xh,
        TEXT_COLS,
    )

    shared_cols = C_MOD + C_QKV + C_CQ + C_TEXT
    grads = jnp.concatenate((grads_one[:, :shared_cols], grads_two[:, :C_UP]), axis=1)
    grads = grads.reshape(2, 16, shared_cols + C_UP)
    got = swap_core(pick(grads, 1 - core, 0).astype(BF)).astype(F32)
    kept_cols = pick(grads, core, 0)
    by_core = in_order(core, kept_cols, got, 0)
    at = 0
    pieces = []
    for width in (C_MOD, C_QKV, C_CQ, C_TEXT, C_UP):
        pieces.append(by_core[:, :, at : at + width])
        at += width
    mod_g, qkv_g, cq_g, text_g, up_g = pieces
    mod_wgrad = mod_g.reshape(2, 16, 2, 512).transpose(1, 2, 0, 3).reshape(16, 2 * D)
    qkv_wgrad = qkv_g.reshape(2, 16, 3, 512).transpose(1, 2, 0, 3).reshape(16, 3, D)
    cq_wgrad = cq_g.transpose(1, 0, 2).reshape(16, D)
    text_wgrad = text_g[:, :12].reshape(2, 12, 2, 256).transpose(1, 2, 0, 3).reshape(12, 2, 512)
    gains_grad = kept_cols[12:14, C_MOD + C_QKV + C_CQ : C_MOD + C_QKV + C_CQ + 16]
    up_wgrad = up_g.reshape(2, 16, 32, 64).transpose(1, 2, 0, 3).reshape(16, FF)
    proj_wgrad = rows_as_halves(grads_one[:, shared_cols : shared_cols + C_PROJ])
    co_wgrad = rows_as_halves(grads_one[:, shared_cols + C_PROJ :])
    down_g = grads_two[:, C_UP:]
    down_wgrad = jnp.concatenate((down_g[:, :D], down_g[:, D:]), axis=0)

    small = jnp.concatenate((noise_part[:, None], jnp.pad(text_part, ((0, 0), (0, 0), (0, D - TEXT_W)))), axis=1)
    small = pick(small, core, 0) + swap_core(pick(small, 1 - core, 0))
    small = small + swap_seq(small)
    return (
        block_out,
        tokens_grad,
        small[:1],
        small[None, 1:, :TEXT_W],
        mod_wgrad,
        qkv_wgrad,
        proj_wgrad,
        cq_wgrad,
        text_wgrad,
        co_wgrad,
        gains_grad,
        up_wgrad,
        down_wgrad,
    )


def solution(mesh):
    split = Mesh(mesh.devices.reshape(SIZES), AXES)
    in_specs = (
        P(FSDP, "xl", None),
        P(FSDP, None),
        P(FSDP, None, None),
        P(FSDP),
        P(FSDP, None),
        P(FSDP, None, None),
        P(FSDP, None),
        P(FSDP, None),
        P(FSDP, None, "xl"),
        P(FSDP, None),
        P(None, FSDP),
        P(FSDP, None),
        P(FSDP, None),
        P(FSDP, "xl", None),
    )
    out_specs = (
        P(FSDP, "xl", None),
        P(FSDP, "xl", None),
        P(FSDP, None),
        P(FSDP, None, None),
        P(FSDP, None),
        P(FSDP, None, None),
        P(FSDP, None),
        P(FSDP, None),
        P(FSDP, None, "xl"),
        P(FSDP, None),
        P(None, FSDP),
        P(FSDP, None),
        P(FSDP, None),
    )
    return jax.shard_map(
        per_device, mesh=split, in_specs=in_specs, out_specs=out_specs, check_vma=False
    )
```

time: 498 us -> 409 us (0.82)
  local copies, waits for them, and re-layouts: 151 us -> 33.5 us
  Pallas kernels: 0 us -> 67.7 us
  matrix products: 67.6 us -> 6.76 us
  waiting for transfers between devices: 165 us -> 213 us
  other arithmetic: 55.1 us -> 29.3 us
    pallas_call x0 -> x10, Pallas kernels: none -> 67.7 us  [call(): pl.pallas_call(body, out_shape=outs, grid_spec=pltpu.PrefetchScalarGridSp...]
    dot_general x33 -> x1, matrix products: 65.9 us -> 5.84 us  [per_device(): jnp.einsum('ic,zyxrc->izxyr', mod_half, mod_w, precision=HIGHEST_PREC)]
    reshape x8 -> x0, local copies, waits for them, and re-layouts: 37.3 us -> none  [the longest x2 16.1 us: gather_chips(): full = full.reshape(4, 4, 2, 32, cols)]
    all_gather x2, waiting for transfers between devices: 64.5 us -> 86.9 us  [gather_chips(): full = lax.all_gather(pair, ('z', 'y'), axis=0, tiled=False)]
    reduce_scatter x2, waiting for transfers between devices: 52.6 us -> 72.9 us  [scatter_chips(): lax.psum_scatter(full.reshape(D, cols), ('z', 'y'), scatter_dimension=0,...]
    transpose x4 -> x5, local copies, waits for them, and re-layouts: 21.7 us -> 2.52 us  [the longest x2 2.39 us: per_device(): full_one[..., TEXT_COLS[0]:TEXT_COLS[1]].transpose(0, 2, 1, 3, 4)]
    unnamed x203 -> x63, local copies, waits for them, and re-layouts: 25.1 us -> 6.88 us
    slice x15 -> x2, local copies, waits for them, and re-layouts: 19.2 us -> 1.83 us  [the longest x1 0.91 us: per_device(): tok = both[:, :rows].reshape(256, D)]
  transfers between devices with their start and end apart: 34 -> 34, of which waited for: 17 -> 17; matrix products, arithmetic and copies ran while one was open for 42% -> 13% of each run, Pallas kernels for 0% -> 13%
where the time goes in v2:
time: 409 us; the launch traced here: 401 us
  waiting for transfers between devices  213 us (52%)
  Pallas kernels  67.7 us (17%)
  starting transfers between devices  34.7 us (8%)
  local copies, waits for them, and re-layouts  33.5 us (8%)
  other arithmetic  29.3 us (7%)
  between operations  15.8 us (4%)
  matrix products  6.76 us (2%)
    all_gather x2, waiting for transfers between devices, gather_chips(): full = lax.all_gather(pair, ('z', 'y'), axis=0, tiled=False)  86.9 us
    reduce_scatter x2, waiting for transfers between devices, scatter_chips(): lax.psum_scatter(full.reshape(D, cols), ('z', 'y'), scatter_dimension=0,...  72.9 us
    pallas_call x10, Pallas kernels, call(): pl.pallas_call(body, out_shape=outs, grid_spec=pltpu.PrefetchScalarGridSp...  67.7 us
    ppermute x9, waiting for transfers between devices, swap_x(): lax.ppermute(value, RING_X, [p for a, b in pairs for p in ((a, b), (b, a))])  31.8 us
    ppermute x16, starting transfers between devices, swap_core(): return lax.ppermute(value, 'core', [(0, 1), (1, 0)])  15.1 us
    ppermute x5, waiting for transfers between devices, swap_seq(): return lax.ppermute(value, 'xl', [(0, 1), (1, 0)])  13 us
    ppermute x9, starting transfers between devices, swap_x(): lax.ppermute(value, RING_X, [p for a, b in pairs for p in ((a, b), (b, a))])  13 us
    select_n x13, other arithmetic, pick(): jnp.where(index == 0, lax.index_in_dim(value, 0, axis, False), lax.index_...  8.47 us
  transfers between devices with their start and end apart: 34, of which 17 were waited for; matrix products, arithmetic and copies ran while one was open for 13% of the time, Pallas kernels for 13%

profile of v2, /device:TPU:1, one launch (start us, length us, event | category | flops | bytes accessed | tf_op | source)
XLA Modules:
  0.0 401.0 jit_solution(17044581136951249645)
XLA Ops:
  15.3 2.6 collective-permute-start.2
  18.5 7.0 %collective-permute-done.2 = bf16[32,4608]{1,0:T(8,128)(2,1)S(1)} collective-permute-done((bf16[32,4608]{1,0:T(8,128)(2,1)S(1)}, bf16[32,4608]{1,0:T(8,128)(2,1)S(1)}, u32[]{:S(2)}, u32[]{:S(2)}) %collective-permute-start.2) | collective-permute-done | bytes 294944 | tf_op jit(solution)/shard_map/ppermute | solution.py:546
  26.6 2.9 collective-permute-start.11
  29.5 5.3 %collective-permute-done.11 = bf16[32,4096]{1,0:T(8,128)(2,1)S(1)} collective-permute-done((bf16[32,4096]{1,0:T(8,128)(2,1)S(1)}, bf16[32,4096]{1,0:T(8,128)(2,1)S(1)}, u32[]{:S(2)}, u32[]{:S(2)}) %collective-permute-start.11) | collective-permute-done | bytes 262176 | tf_op jit(solution)/shard_map/ppermute | solution.py:546
  42.3 62.8 %all-gather.5.cloned.1.call-done = bf16[32,32,4608]{2,1,0:T(8,128)(2,1)} async-done(((bf16[2,32,4608]{2,1,0:T(8,128)(2,1)}), bf16[32,32,4608]{2,1,0:T(8,128)(2,1)}) %all-gather.5.cloned.1.call-update) | async-done | bytes 9437200 | tf_op jit(solution)/shard_map/all_gather | solution.py:574
  105.1 3.0 broadcast_select_fusion
  114.7 4.1 %shard_map.238 = (bf16[256,1024]{1,0:T(8,128)(2,1)}, bf16[256,512]{1,0:T(8,128)(2,1)}, bf16[256,1024]{1,0:T(8,128)(2,1)}) custom-call(bf16[256,1024]{1,0:T(8,128)(2,1)} %bitcast.188, f32[2,1024]{1,0:T(2,128)} %get-tuple-element.143.scale, f32[2,1024]{1,0:T(2,128)} %get-tuple-element.142.shift, bf16[4,4,2,32,4608]{4,3,2,1,0:T(8,128)(2,1)} %bitcast.174, ...), custom_call_target="tpu_custom_call" | custom-call | tf_op jit(solution)/shard_map/pallas_call | solution.py:75
  125.2 3.0 shard_map.239
  128.2 4.3 %collective-permute-done.5.kv_far = bf16[256,1024]{1,0:T(8,128)(2,1)} collective-permute-done((bf16[256,1024]{1,0:T(8,128)(2,1)}, bf16[256,1024]{1,0:T(8,128)(2,1)}, u32[]{:S(2)}, u32[]{:S(2)}) %collective-permute-start.5) | collective-permute-done | bytes 524320 | tf_op jit(solution)/shard_map/ppermute | solution.py:542
  132.6 6.0 %shard_map.240 = (bf16[256,512]{1,0:T(8,128)(2,1)}, f32[256,1024]{1,0:T(8,128)}) custom-call(bf16[256,512]{1,0:T(8,128)(2,1)} %get-tuple-element.45.q, bf16[256,1024]{1,0:T(8,128)(2,1)} %get-tuple-element.46.kv, bf16[256,1024]{1,0:T(8,128)(2,1)} %collective-permute-done.5.kv_far, bf16[512,1024]{1,0:T(8,128)(2,1)} %get-tuple-element.47.proj_w), custom_call_target="tpu_custom_call" | custom-call | tf_op jit(solution)/shard_map/pallas_call | solution.py:75
  146.2 5.3 %shard_map.241 = (f32[256,1024]{1,0:T(8,128)}, bf16[256,1024]{1,0:T(8,128)(2,1)}, bf16[256,512]{1,0:T(8,128)(2,1)}, bf16[256,512]{1,0:T(8,128)(2,1)}, f32[256,1024]{1,0:T(8,128)}) custom-call(bf16[256,1024]{1,0:T(8,128)(2,1)} %bitcast.189, f32[256,1024]{1,0:T(8,128)} %get-tuple-element.48.part, f32[256,1024]{1,0:T(8,128)} %collective-permute-done.7.part_far, ...), custom_call_target="tpu_custom_call" | custom-call | tf_op jit(solution)/shard_map/pallas_call | solution.py:75
  153.6 24.1 %all-gather.7.cloned.1.call-done = bf16[32,32,4096]{2,1,0:T(8,128)(2,1)} async-done(((bf16[2,32,4096]{2,1,0:T(8,128)(2,1)}), bf16[32,32,4096]{2,1,0:T(8,128)(2,1)}) %all-gather.7.cloned.1.call-update) | async-done | bytes 8388624 | tf_op jit(solution)/shard_map/all_gather | solution.py:574
  177.7 15.7 %shard_map.242 = (f32[256,1024]{1,0:T(8,128)}, bf16[4,4,2,32,4096]{4,3,2,1,0:T(8,128)(2,1)}, f32[256,1024]{1,0:T(8,128)}, f32[256,1024]{1,0:T(8,128)}) custom-call(f32[256,1024]{1,0:T(8,128)} %get-tuple-element.50.res, f32[256,1024]{1,0:T(8,128)} %get-tuple-element.51.part, f32[256,1024]{1,0:T(8,128)} %collective-permute-done.10.part_far, ...), custom_call_target="tpu_custom_call" | custom-call | tf_op jit(solution)/shard_map/pallas_call | solution.py:75
  197.0 7.8 %shard_map.243 = (f32[256,1024]{1,0:T(8,128)}, f32[1,1024]{1,0:T(1,128)}, bf16[512,1024]{1,0:T(8,128)(2,1)}, bf16[4,4,2,32,512]{4,3,2,1,0:T(8,128)(2,1)}, f32[2,8,1024]{2,1,0:T(8,128)}, /*index=5*/f32[256,1024]{1,0:T(8,128)}) custom-call(f32[256,1024]{1,0:T(8,128)} %get-tuple-element.54.part, f32[256,1024]{1,0:T(8,128)} %collective-permute-done.13.part_far, ...), custom_call_target="tpu_custom_call" | custom-call | tf_op jit(solution)/shard_map/pallas_call | solution.py:75
  208.9 13.5 %shard_map.244 = (f32[256,1024]{1,0:T(8,128)}, f32[1,1024]{1,0:T(1,128)}, bf16[512,1024]{1,0:T(8,128)(2,1)}, bf16[256,512]{1,0:T(8,128)(2,1)}, f32[256,1024]{1,0:T(8,128)}, /*index=5*/bf16[256,1024]{1,0:T(8,128)(2,1)}) custom-call(f32[256,1024]{1,0:T(8,128)} %get-tuple-element.58.part, f32[256,1024]{1,0:T(8,128)} %collective-permute-done.14.part_far, ...), custom_call_target="tpu_custom_call" | custom-call | tf_op jit(solution)/shard_map/pallas_call | solution.py:75
  225.8 3.3 shard_map.246
  229.5 5.6 %collective-permute-done.15.dfar = bf16[256,1024]{1,0:T(8,128)(2,1)S(1)} collective-permute-done((bf16[256,1024]{1,0:T(8,128)(2,1)}, bf16[256,1024]{1,0:T(8,128)(2,1)S(1)}, u32[]{:S(2)}, u32[]{:S(2)}) %collective-permute-start.15) | collective-permute-done | bytes 524320 | tf_op jit(solution)/shard_map/ppermute | solution.py:542
  235.9 6.5 %shard_map.245 = (bf16[4,4,2,32,1536]{4,3,2,1,0:T(8,128)(2,1)}, f32[256,1024]{1,0:T(8,128)}) custom-call(bf16[256,512]{1,0:T(8,128)(2,1)} %get-tuple-element.62.dq, f32[256,1024]{1,0:T(8,128)} %get-tuple-element.63.dkv, bf16[256,1024]{1,0:T(8,128)(2,1)} %copy-done.9, bf16[256,1024]{1,0:T(8,128)(2,1)} %get-tuple-element.65.n1, ...), custom_call_target="tpu_custom_call" | custom-call | tf_op jit(solution)/shard_map/pallas_call | solution.py:75
  248.2 3.3 reshape.476
  270.2 5.8 %fusion.4 = f32[2,4,2,4,32]{4,0,2,3,1:T(2,128)S(1)} fusion(bf16[4,4,2,32,4608]{4,3,2,1,0:T(8,128)(2,1)} %bitcast.183, f32[2,1024,1,1,1]{1,0,2,3,4:T(2,128)S(1)} %reshape.498), kind=kOutput, calls=%fused_computation.9 | convolution fusion | flops 25165824 | bytes 2113536 | tf_op jit(solution)/shard_map/ic,zyxrc->izxyr/dot_general | solution.py:735
  285.7 8.8 %collective-permute-done.27 = bf16[32,4096]{1,0:T(8,128)(2,1)S(1)} collective-permute-done((bf16[32,4096]{1,0:T(8,128)(2,1)S(1)}, bf16[32,4096]{1,0:T(8,128)(2,1)S(1)}, u32[]{:S(2)}, u32[]{:S(2)}) %collective-permute-start.27) | collective-permute-done | bytes 262176 | tf_op jit(solution)/shard_map/ppermute | solution.py:546
  294.6 72.9 %reduce-scatter.3.cloned.1.call-done = bf16[64,4608]{1,0:T(8,128)(2,1)} async-done(((bf16[1024,4608]{1,0:T(8,128)(2,1)}), bf16[64,4608]{1,0:T(8,128)(2,1)}) %reduce-scatter.3.cloned.1.call-update) | async-done | bytes 589840 | tf_op jit(solution)/shard_map/reduce_scatter | solution.py:581
  372.7 10.8 %collective-permute-done.24 = bf16[32,4608]{1,0:T(8,128)(2,1)S(1)} collective-permute-done((bf16[32,4608]{1,0:T(8,128)(2,1)S(1)}, bf16[32,4608]{1,0:T(8,128)(2,1)S(1)}, u32[]{:S(2)}, u32[]{:S(2)}) %collective-permute-start.24) | collective-permute-done | bytes 294944 | tf_op jit(solution)/shard_map/ppermute | solution.py:546
  383.9 2.9 collective-permute-start.29
  (261 shorter events, 98.0 us)
Async XLA Ops:
  7.2 97.9 %all-gather.5.cloned.1.call-start = ((), (), s32[]{:S(2)}) async-start(), calls=%async_computation.4 | async-start | bytes 10027008 | tf_op jit(solution)/shard_map/all_gather | solution.py:574
  15.3 10.2 %collective-permute-start.2 = (bf16[32,4608]{1,0:T(8,128)(2,1)S(1)}, bf16[32,4608]{1,0:T(8,128)(2,1)S(1)}, u32[]{:S(2)}, u32[]{:S(2)}) collective-permute-start(bf16[32,4608]{1,0:T(8,128)(2,1)S(1)} %maximum_maximum_fusion), channel_id=1, source_target_pairs={{0,17},{17,0},{1,16},{16,1},{2,19},{19,2},{3,18},{18,3},{4,21},{21... | collective-permute-start | bytes 884744 | tf_op jit(solution)/shard_map/ppermute | solution.py:546
  17.9 7.6 %collective-permute-start.3 = (bf16[32,512]{1,0:T(8,128)(2,1)S(1)}, bf16[32,512]{1,0:T(8,128)(2,1)S(1)}, u32[]{:S(2)}, u32[]{:S(2)}) collective-permute-start(bf16[32,512]{1,0:T(8,128)(2,1)S(1)} %fusion.28), channel_id=1, source_target_pairs={{0,16},{16,0},{1,17},{17,1},{2,18},{18,2},{3,19},{19,3},{4,20},{20... | collective-permute-start | bytes 98312 | tf_op jit(solution)/shard_map/ppermute | solution.py:546
  26.5 151.2 %all-gather.7.cloned.1.call-start = ((), (), s32[]{:S(2)}) async-start(), calls=%async_computation.5 | async-start | bytes 8912896 | tf_op jit(solution)/shard_map/all_gather | solution.py:574
  26.6 8.1 %collective-permute-start.11 = (bf16[32,4096]{1,0:T(8,128)(2,1)S(1)}, bf16[32,4096]{1,0:T(8,128)(2,1)S(1)}, u32[]{:S(2)}, u32[]{:S(2)}) collective-permute-start(bf16[32,4096]{1,0:T(8,128)(2,1)S(1)} %fusion.22), channel_id=1, source_target_pairs={{0,17},{17,0},{1,16},{16,1},{2,19},{19,2},{3,18},{18,3},{4,21},{21... | collective-permute-start | bytes 786440 | tf_op jit(solution)/shard_map/ppermute | solution.py:546
  35.7 243.1 %reduce-scatter.5.cloned.1.call-start = ((), (), s32[]{:S(2)}) async-start(), calls=%async_computation.3 | async-start | bytes 8912896 | tf_op jit(solution)/shard_map/reduce_scatter | solution.py:581
  36.8 3.7 collective-permute-start
  108.1 17.1 %collective-permute-start.6 = (bf16[2,4,2,32,1024]{4,3,2,1,0:T(8,128)(2,1)}, bf16[2,4,2,32,1024]{4,3,2,1,0:T(8,128)(2,1)}, u32[]{:S(2)}, u32[]{:S(2)}) collective-permute-start(bf16[2,4,2,32,1024]{4,3,2,1,0:T(8,128)(2,1)} %get-tuple-element.86), channel_id=1, source_target_pairs={{0,2},{2,0},{1,3},{3,1},{4,6},{6,4},{5,7},{7,5},{8,10},{10,8},{9,1... | collective-permute-start | bytes 3145736 | tf_op jit(solution)/shard_map/ppermute | solution.py:538
  118.8 13.7 %collective-permute-start.5 = (bf16[256,1024]{1,0:T(8,128)(2,1)}, bf16[256,1024]{1,0:T(8,128)(2,1)}, u32[]{:S(2)}, u32[]{:S(2)}) collective-permute-start(bf16[256,1024]{1,0:T(8,128)(2,1)} %get-tuple-element.46.kv), channel_id=1, source_target_pairs={{0,1},{1,0},{2,3},{3,2},{4,5},{5,4},{6,7},{7,6},{8,9},{9,8},{10,11... | collective-permute-start | bytes 1572872 | tf_op jit(solution)/shard_map/ppermute | solution.py:542
  138.5 7.7 %collective-permute-start.7 = (f32[256,1024]{1,0:T(8,128)}, f32[256,1024]{1,0:T(8,128)}, u32[]{:S(2)}, u32[]{:S(2)}) collective-permute-start(f32[256,1024]{1,0:T(8,128)} %get-tuple-element.48.part), channel_id=1, source_target_pairs={{0,2},{2,0},{1,3},{3,1},{4,6},{6,4},{5,7},{7,5},{8,10},{10,8},{9,1... | collective-permute-start | bytes 3145736 | tf_op jit(solution)/shard_map/ppermute | solution.py:538
  151.5 26.2 %collective-permute-start.10 = (f32[256,1024]{1,0:T(8,128)}, f32[256,1024]{1,0:T(8,128)}, u32[]{:S(2)}, u32[]{:S(2)}) collective-permute-start(f32[256,1024]{1,0:T(8,128)} %get-tuple-element.51.part), channel_id=1, source_target_pairs={{0,2},{2,0},{1,3},{3,1},{4,6},{6,4},{5,7},{7,5},{8,10},{10,8},{9,1... | collective-permute-start | bytes 3145736 | tf_op jit(solution)/shard_map/ppermute | solution.py:538
  193.4 174.2 %reduce-scatter.3.cloned.1.call-start = ((), (), s32[]{:S(2)}) async-start(), calls=%async_computation.2 | async-start | bytes 10027008 | tf_op jit(solution)/shard_map/reduce_scatter | solution.py:581
  204.9 4.0 %collective-permute-start.14 = (f32[256,1024]{1,0:T(8,128)}, f32[256,1024]{1,0:T(8,128)}, u32[]{:S(2)}, u32[]{:S(2)}) collective-permute-start(f32[256,1024]{1,0:T(8,128)} %get-tuple-element.58.part), channel_id=1, source_target_pairs={{0,2},{2,0},{1,3},{3,1},{4,6},{6,4},{5,7},{7,5},{8,10},{10,8},{9,1... | collective-permute-start | bytes 3145736 | tf_op jit(solution)/shard_map/ppermute | solution.py:538
  222.4 12.7 %collective-permute-start.15 = (bf16[256,1024]{1,0:T(8,128)(2,1)}, bf16[256,1024]{1,0:T(8,128)(2,1)S(1)}, u32[]{:S(2)}, u32[]{:S(2)}) collective-permute-start(bf16[256,1024]{1,0:T(8,128)(2,1)} %get-tuple-element.64), channel_id=1, source_target_pairs={{0,1},{1,0},{2,3},{3,2},{4,5},{5,4},{6,7},{7,6},{8,9},{9,8},{10,11... | collective-permute-start | bytes 1572872 | tf_op jit(solution)/shard_map/ppermute | solution.py:542
  229.1 24.7 %collective-permute-start.22 = (bf16[2,4,2,32,1024]{4,3,2,1,0:T(8,128)(2,1)}, bf16[2,4,2,32,1024]{4,3,2,1,0:T(8,128)(2,1)}, u32[]{:S(2)}, u32[]{:S(2)}) collective-permute-start(bf16[2,4,2,32,1024]{4,3,2,1,0:T(8,128)(2,1)} %get-tuple-element.75), channel_id=1, source_target_pairs={{0,2},{2,0},{1,3},{3,1},{4,6},{6,4},{5,7},{7,5},{8,10},{10,8},{9,1... | collective-permute-start | bytes 3145736 | tf_op jit(solution)/shard_map/ppermute | solution.py:538
  244.4 8.9 %collective-permute-start.16 = (f32[128,1024]{1,0:T(8,128)}, f32[128,1024]{1,0:T(8,128)S(1)}, u32[]{:S(2)}, u32[]{:S(2)}) collective-permute-start(f32[128,1024]{1,0:T(8,128)} %slice_select_fusion), channel_id=1, source_target_pairs={{0,2},{2,0},{1,3},{3,1},{4,6},{6,4},{5,7},{7,5},{8,10},{10,8},{9,1... | collective-permute-start | bytes 1572872 | tf_op jit(solution)/shard_map/ppermute | solution.py:538
  277.6 6.9 %collective-permute-start.21 = (f32[9,1024]{1,0:T(8,128)S(1)}, f32[9,1024]{1,0:T(8,128)S(1)}, u32[]{:S(2)}, u32[]{:S(2)}) collective-permute-start(f32[9,1024]{1,0:T(8,128)S(1)} %bitcast_add_fusion), channel_id=1, source_target_pairs={{0,1},{1,0},{2,3},{3,2},{4,5},{5,4},{6,7},{7,6},{8,9},{9,8},{10,11... | collective-permute-start | bytes 110600 | tf_op jit(solution)/shard_map/ppermute | solution.py:542
  279.9 14.6 %collective-permute-start.28 = (bf16[32,4096]{1,0:T(8,128)(2,1)S(1)}, bf16[32,4096]{1,0:T(8,128)(2,1)S(1)}, u32[]{:S(2)}, u32[]{:S(2)}) collective-permute-start(bf16[32,4096]{1,0:T(8,128)(2,1)S(1)} %get-tuple-element.105), channel_id=1, source_target_pairs={{0,17},{17,0},{1,16},{16,1},{2,19},{19,2},{3,18},{18,3},{4,21},{21... | collective-permute-start | bytes 786440 | tf_op jit(solution)/shard_map/ppermute | solution.py:546
  281.8 12.7 %collective-permute-start.26 = (bf16[32,4096]{1,0:T(8,128)(2,1)S(1)}, bf16[32,4096]{1,0:T(8,128)(2,1)S(1)}, u32[]{:S(2)}, u32[]{:S(2)}) collective-permute-start(bf16[32,4096]{1,0:T(8,128)(2,1)S(1)} %get-tuple-element.105), channel_id=1, source_target_pairs={{0,16},{16,0},{1,17},{17,1},{2,18},{18,2},{3,19},{19,3},{4,20},{20... | collective-permute-start | bytes 786440 | tf_op jit(solution)/shard_map/ppermute | solution.py:546
  282.5 12.0 %collective-permute-start.27 = (bf16[32,4096]{1,0:T(8,128)(2,1)S(1)}, bf16[32,4096]{1,0:T(8,128)(2,1)S(1)}, u32[]{:S(2)}, u32[]{:S(2)}) collective-permute-start(bf16[32,4096]{1,0:T(8,128)(2,1)S(1)} %get-tuple-element.104), channel_id=1, source_target_pairs={{0,1},{1,0},{16,17},{17,16},{2,3},{3,2},{18,19},{19,18},{4,5},{5,4... | collective-permute-start | bytes 786440 | tf_op jit(solution)/shard_map/ppermute | solution.py:546
  368.7 14.9 %collective-permute-start.25 = (bf16[32,4608]{1,0:T(8,128)(2,1)S(1)}, bf16[32,4608]{1,0:T(8,128)(2,1)S(1)}, u32[]{:S(2)}, u32[]{:S(2)}) collective-permute-start(bf16[32,4608]{1,0:T(8,128)(2,1)S(1)} %get-tuple-element.99), channel_id=1, source_target_pairs={{0,17},{17,0},{1,16},{16,1},{2,19},{19,2},{3,18},{18,3},{4,21},{21... | collective-permute-start | bytes 884744 | tf_op jit(solution)/shard_map/ppermute | solution.py:546
  371.1 12.4 %collective-permute-start.23 = (bf16[32,4608]{1,0:T(8,128)(2,1)S(1)}, bf16[32,4608]{1,0:T(8,128)(2,1)S(1)}, u32[]{:S(2)}, u32[]{:S(2)}) collective-permute-start(bf16[32,4608]{1,0:T(8,128)(2,1)S(1)} %get-tuple-element.99), channel_id=1, source_target_pairs={{0,16},{16,0},{1,17},{17,1},{2,18},{18,2},{3,19},{19,3},{4,20},{20... | collective-permute-start | bytes 884744 | tf_op jit(solution)/shard_map/ppermute | solution.py:546
  371.7 11.8 %collective-permute-start.24 = (bf16[32,4608]{1,0:T(8,128)(2,1)S(1)}, bf16[32,4608]{1,0:T(8,128)(2,1)S(1)}, u32[]{:S(2)}, u32[]{:S(2)}) collective-permute-start(bf16[32,4608]{1,0:T(8,128)(2,1)S(1)} %get-tuple-element.98), channel_id=1, source_target_pairs={{0,1},{1,0},{16,17},{17,16},{2,3},{3,2},{18,19},{19,18},{4,5},{5,4... | collective-permute-start | bytes 884744 | tf_op jit(solution)/shard_map/ppermute | solution.py:546
  383.9 4.1 %collective-permute-start.29 = (bf16[16,5632]{1,0:T(8,128)(2,1)S(1)}, bf16[16,5632]{1,0:T(8,128)(2,1)S(1)}, u32[]{:S(2)}, u32[]{:S(2)}) collective-permute-start(bf16[16,5632]{1,0:T(8,128)(2,1)S(1)} %select_convert_fusion), channel_id=1, source_target_pairs={{0,2},{2,0},{1,3},{3,1},{4,6},{6,4},{5,7},{7,5},{8,10},{10,8},{9,1... | collective-permute-start | bytes 540680 | tf_op jit(solution)/shard_map/ppermute | solution.py:538
  (32 other events, 160.7 us)
Sparse Core Ops, SparseCore 0:
  26.7 78.4 all-gather.4
  107.2 70.4 all-gather.6
  193.5 83.6 reduce-scatter.4
  280.5 86.9 reduce-scatter.2

commit v3 on v2

--- a/solution.py
+++ b/solution.py
@@ -24,8 +24,8 @@
 TXT = 8
 CHIPS = 32
 
-C_MOD, C_QKV, C_CQ, C_TEXT, C_PROJ, C_CO = 1024, 1536, 512, 512, 512, 512
-TEXT_COLS = (C_MOD + C_QKV + C_CQ, C_MOD + C_QKV + C_CQ + C_TEXT)
+C_QKV, C_CQ, C_TEXT, C_PROJ, C_CO = 1536, 512, 512, 512, 512
+TEXT_COLS = (C_QKV + C_CQ, C_QKV + C_CQ + C_TEXT)
 C_UP, C_DOWN = 2048, 2048
 
 
@@ -102,21 +102,6 @@
     return pl.BlockSpec(dims, lambda i: (0,) * len(dims))
 
 
-def mod_body(noise, w, out):
-    out[...] = mm(noise[...], nat(w))
-
-
-def mod_kernel(noise, full):
-    return call(
-        mod_body,
-        [shape((2, 1024), F32)],
-        (noise, full),
-        specs=[fixed((2, D)), cols_spec(0, 1024)],
-        out_specs=[fixed((2, 1024))],
-        grid=(1,),
-    )[0]
-
-
 def qkv_body(tok, scale, shift, wq, wk, wv, n1_out, q_out, kv_out):
     for b in range(2):
         r = slice(128 * b, 128 * b + 128)
@@ -133,7 +118,7 @@
         qkv_body,
         [shape((256, D), BF), shape((256, 512), BF), shape((256, D), BF)],
         (tok, scale, shift, full, full, full),
-        specs=[fixed((256, D)), fixed((2, D)), fixed((2, D)), cols_spec(2), cols_spec(3), cols_spec(4)],
+        specs=[fixed((256, D)), fixed((2, D)), fixed((2, D)), cols_spec(0), cols_spec(1), cols_spec(2)],
         out_specs=[fixed((256, D)), fixed((256, 512)), fixed((256, D))],
         grid=(1,),
     )
@@ -233,7 +218,7 @@
             f((256, D)),
             f((256, D)),
             f((2, D)),
-            cols_spec(5),
+            cols_spec(3),
             f((2, 8, D)),
             SMEM,
             f((512, D)),
@@ -383,7 +368,7 @@
             f((2, 8, D)),
             SMEM,
             f((512, D)),
-            cols_spec(5),
+            cols_spec(3),
         ],
         out_specs=[
             f((256, D)),
@@ -471,13 +456,61 @@
             f((256, D)),
             f((256, D)),
             f((256, D)),
+            cols_spec(0),
+            cols_spec(1),
             cols_spec(2),
-            cols_spec(3),
-            cols_spec(4),
         ],
         out_specs=[f((4, 4, 2, 32, 1536)), f((256, D))],
         grid=(1,),
     )
+
+
+def sum_body(*refs):
+    total = refs[0][...].astype(F32)
+    for r in refs[1:-1]:
+        total = total + r[...].astype(F32)
+    refs[-1][...] = total.astype(refs[-1].dtype)
+
+
+def sum_kernel(*pieces):
+    return call(sum_body, [shape(pieces[0].shape, BF)], pieces)[0]
+
+
+LATE = C_QKV + C_TEXT + C_CQ + C_PROJ + C_CO
+LATE_ROWS = LATE - C_PROJ - C_CO
+
+
+def late_body(ids, text, qkv, cq, kept, came, out):
+    out[:, :, :, :, :C_QKV] = qkv[...]
+    at = C_QKV + C_TEXT
+    out[:, :, :, :, C_QKV:at] = text[...]
+    out[:, :, :, :, at : at + C_CQ] = cq[...]
+    first = ids[0] == 0
+    a, b = kept[...], came[...]
+    out[:2, :, :, :, LATE_ROWS:] = jnp.where(first, a, b)
+    out[2:, :, :, :, LATE_ROWS:] = jnp.where(first, b, a)
+
+
+def late_kernel(ids, text, qkv, cq, kept, came):
+    return call(
+        late_body,
+        [shape((4, 4, 2, 32, LATE), BF)],
+        (ids, text, qkv, cq, kept, came),
+        specs=[SMEM, *[WHOLE] * 5],
+    )[0]
+
+
+def late_sum_body(own, a, b, e, out):
+    near = a[...].astype(F32) + b[...].astype(F32)
+    row = lax.broadcasted_iota(jnp.int32, near.shape, 0) % 16
+    col = lax.broadcasted_iota(jnp.int32, near.shape, 1)
+    text = (col >= C_QKV) & (col < C_QKV + C_TEXT)
+    near = jnp.where((row < 12) & text, 0.0, near)
+    out[...] = (own[...].astype(F32) + e[...].astype(F32) + near).astype(BF)
+
+
+def late_sum_kernel(own, a, b, e):
+    return call(late_sum_body, [shape((32, LATE), BF)], (own, a, b, e))[0]
 
 
 def rows_body(core, kept, came, proj_out, co_out):
@@ -534,6 +567,52 @@
     )
 
 
+def ff_unpack_body(ids, mine, came, down, up_out, down_out):
+    first = ids[0] == 0
+    a, b = mine[...].astype(F32), came[...].astype(F32)
+    parts = (jnp.where(first, a, b), jnp.where(first, b, a))
+    for i in range(32):
+        for c in range(2):
+            to = 128 * i + 64 * c
+            up_out[:, to : to + 64] = parts[c][:, 64 * i : 64 * i + 64]
+    down_out[:32] = down[:, :D].astype(F32)
+    down_out[32:] = down[:, D:].astype(F32)
+
+
+def ff_unpack_kernel(ids, mine, came, down):
+    return call(
+        ff_unpack_body,
+        [shape((16, FF), F32), shape((64, D), F32)],
+        (ids, mine, came, down),
+        specs=[SMEM, WHOLE, WHOLE, WHOLE],
+    )
+
+
+def late_unpack_body(ids, mine, came, rows, qkv_out, cq_out, proj_out, co_out):
+    first = ids[0] == 0
+    a, b = mine[...].astype(F32), came[...].astype(F32)
+    parts = (jnp.where(first, a, b), jnp.where(first, b, a))
+    for c in range(2):
+        to = slice(512 * c, 512 * c + 512)
+        for i in range(3):
+            qkv_out[i, :, to] = parts[c][:, 512 * i : 512 * i + 512]
+        cq_out[:, to] = parts[c][:, LATE_ROWS - 512 : LATE_ROWS]
+    for i, out in enumerate((proj_out, co_out)):
+        for h in range(2):
+            out[:, 512 * h : 512 * h + 512] = rows[
+                16 * h : 16 * h + 16, 512 * i : 512 * i + 512
+            ].astype(F32)
+
+
+def late_unpack_kernel(ids, mine, came, rows):
+    return call(
+        late_unpack_body,
+        [shape((3, 16, D), F32), shape((16, D), F32), shape((16, D), F32), shape((16, D), F32)],
+        (ids, mine, came, rows),
+        specs=[SMEM, WHOLE, WHOLE, WHOLE],
+    )
+
+
 def swap_core(value):
     return lax.ppermute(value, "core", [(0, 1), (1, 0)])
 
@@ -564,44 +643,30 @@
     )
 
 
-def gather_chips(block, xh, text_cols=None):
-    other = swap_x(block, ((0, 3), (1, 2)))
-    if text_cols is not None:
-        lo, hi = text_cols
-        far = swap_x(block[:, lo:hi], ((0, 2), (1, 3)))
-        other = jnp.concatenate((other[:, :lo], far, other[:, hi:]), axis=1)
+def gather_chips(block, other, xh):
     pair = in_order(xh, block, other, 0)
     full = lax.all_gather(pair, ("z", "y"), axis=0, tiled=False)
     cols = block.shape[-1]
     return full.reshape(4, 4, 2, 32, cols)
 
 
-def scatter_chips(full, xh, text_cols=None):
+def ring(value, axis, size, step):
+    return lax.ppermute(value, axis, [(i, (i + step) % size) for i in range(size)])
+
+
+def exchange(value, axes):
+    return lax.all_to_all(value, axes, 0, 0, tiled=True)
+
+
+def zy_scatter(full):
     cols = full.shape[-1]
     part = lax.psum_scatter(full.reshape(D, cols), ("z", "y"), scatter_dimension=0, tiled=True)
-    part = part.reshape(2, 32, cols)
-    own = pick(part, xh, 0)
-    far = pick(part, 1 - xh, 0)
-    a = swap_x(own, ((0, 1), (2, 3)))
-    b = swap_x(far, ((0, 3), (1, 2)))
-    e = swap_x(far, ((0, 2), (1, 3)))
-    near = a.astype(F32) + b.astype(F32)
-    if text_cols is not None:
-        col = lax.broadcasted_iota(jnp.int32, near.shape, 1)
-        row = lax.broadcasted_iota(jnp.int32, near.shape, 0)
-        is_text = (col >= text_cols[0]) & (col < text_cols[1]) & (row % 16 < 12)
-        near = jnp.where(is_text, 0.0, near)
-    return (own.astype(F32) + e.astype(F32)) + near
+    return part.reshape(2, 32, cols)
 
 
 def halves_as_rows(value):
     k = value.shape[-1] // 2
     return jnp.concatenate((value[:, :k], value[:, k:]), axis=0)
-
-
-def rows_as_halves(value):
-    r = value.shape[0] // 2
-    return jnp.concatenate((value[:r], value[r:]), axis=1)
 
 
 def per_device(
@@ -627,9 +692,8 @@
 
     misc = jnp.concatenate(
         (
-            noise_emb,
             jnp.pad(text_emb[0], ((0, 0), (0, D - TEXT_W))),
-            jnp.broadcast_to(prompt_len.astype(BF)[:, None], (7, D)),
+            jnp.broadcast_to(prompt_len.astype(BF)[:, None], (8, D)),
         ),
         axis=0,
     )
@@ -637,23 +701,21 @@
     both = in_order(core, mine, swap_core(mine), 0)
     tok = both[:, :rows].reshape(256, D)
     og = both[:, rows : 2 * rows].reshape(256, D)
-    noise = both[:, 2 * rows]
-    text = both[:, 2 * rows + 1 : 2 * rows + 9, :TEXT_W]
-    lens = both[:, 2 * rows + 9, 0].astype(jnp.int32)
+    text = both[:, 2 * rows : 2 * rows + 8, :TEXT_W]
+    lens = both[:, 2 * rows + 8, 0].astype(jnp.int32)
 
     def side(which):
         up = pick(up_weight.reshape(16, 32, 2, 64), which, 2).reshape(16, C_UP)
         qkv = pick(qkv_weight.reshape(16, 3, 2, 512), which, 2).reshape(16, C_QKV)
-        mod = pick(mod_weight.reshape(16, 2, 2, 512), which, 2).reshape(16, C_MOD)
         cq = pick(cq_weight.reshape(16, 2, 512), which, 1)
         txt = pick(text_weight.reshape(12, 2, 2, 256), which, 2).reshape(12, C_TEXT)
         gains = jnp.pad(norm_gains, ((0, 2), (0, C_TEXT - 16)))
-        return jnp.concatenate((mod, qkv, cq, jnp.concatenate((txt, gains), axis=0), up), axis=1)
+        return jnp.concatenate((qkv, cq, jnp.concatenate((txt, gains), axis=0), up), axis=1)
 
     shared = join(core, side(core), swap_core(side(1 - core)), 0)
     first = jnp.concatenate(
         (
-            shared[:, : C_MOD + C_QKV + C_CQ + C_TEXT],
+            shared[:, : C_QKV + C_CQ + C_TEXT],
             halves_as_rows(proj_weight),
             halves_as_rows(co_weight),
         ),
@@ -661,13 +723,19 @@
     )
     second = jnp.concatenate(
         (
-            shared[:, C_MOD + C_QKV + C_CQ + C_TEXT :],
+            shared[:, C_QKV + C_CQ + C_TEXT :],
             jnp.concatenate((down_weight[:32], down_weight[32:]), axis=1),
         ),
         axis=1,
     )
-    full_one = gather_chips(first, xh, TEXT_COLS)
-    full_two = gather_chips(second, xh)
+    near, xl_pair, across = ((0, 3), (1, 2)), ((0, 1), (2, 3)), ((0, 2), (1, 3))
+    lo, hi = TEXT_COLS
+    first_far = swap_x(first, ((0, 3), (1, 2)))
+    text_far = swap_x(first[:, lo:hi], ((0, 2), (1, 3)))
+    second, first_far = lax.optimization_barrier((second, first_far))
+    first_far = jnp.concatenate((first_far[:, :lo], text_far, first_far[:, hi:]), axis=1)
+    full_one = gather_chips(first, first_far, xh)
+    full_two = gather_chips(second, swap_x(second, ((0, 3), (1, 2))), xh)
 
     text_rows = full_one[..., TEXT_COLS[0] : TEXT_COLS[1]].transpose(0, 2, 1, 3, 4)
     text_rows = text_rows.reshape(64, 16, C_TEXT)
@@ -676,10 +744,14 @@
     halves = full_one[..., TEXT_COLS[1] :].reshape(2, 2, 4, 2, 32, D)
     kept = pick(halves, core, 0)
     core_id = core.astype(jnp.int32)[None]
+    y_id = lax.axis_index("y")
+    ids = jnp.stack([core, 2 * xh + xl, y_id, xl]).astype(jnp.int32)
     proj_w, co_w = rows_kernel(core_id, kept, swap_core(pick(halves, 1 - core, 0)))
 
-    mod_part = mod_kernel(noise, full_one).reshape(2, 2, 512)
-    mod_all = join(core, mod_part, swap_core(mod_part), 2)
+    noise_cols = exchange(noise_emb.reshape(64, 16), FSDP)
+    mod_parts = jnp.dot(noise_cols, mod_weight, preferred_element_type=F32)
+    mod_own = jnp.sum(exchange(mod_parts, FSDP), axis=0, keepdims=True)
+    mod_all = in_order(core, mod_own, swap_core(mod_own), 0).reshape(2, 2, D)
     mod_scale, mod_shift = mod_all[:, 0], mod_all[:, 1]
     normed_one, queries, kv_own = qkv_kernel(tok, mod_scale, mod_shift, full_one)
     kv_far = swap_seq(kv_own)
@@ -691,10 +763,10 @@
     after_self, normed_two, cross_q, cross_att, co_part = cross_kernel(
         tok, proj_part, swap_core(proj_part), gains, full_one, text_kv, lens, co_w
     )
-    after_cross, grads_ff, three_part, down_part = ff_kernel(
+    after_cross, ff_wg, three_part, down_part = ff_kernel(
         after_self, co_part, swap_core(co_part), gains, og, full_two
     )
-    grads_two = scatter_chips(grads_ff, xh)
+    ff_sc = zy_scatter(ff_wg)
     down_part = down_part.reshape(2, rows, D)
     down_own = pick(down_part, core, 0) + swap_core(pick(down_part, 1 - core, 0))
     block_out = (pick(after_cross.reshape(2, rows, D), core, 0) + down_own).astype(BF)[None]
@@ -707,7 +779,10 @@
         two_part, swap_core(two_part), after_self, cross_res_grad, gains, attended, queries,
         kv_own, kv_far, proj_w,
     )
-    qkv_wg, one_part = qkv_back_kernel(dq, dkv, swap_seq(dkv_far), normed_one, full_one)
+    rows_kept, rows_sent = rows_back_kernel(core_id, proj_wg, co_wg)
+    dkv_came = swap_seq(dkv_far)
+    rows_came = swap_core(rows_sent)
+    qkv_wg, one_part = qkv_back_kernel(dq, dkv, dkv_came, normed_one, full_one)
 
     text_sum = (text_sum + swap_seq(text_sum.astype(BF)).astype(F32)).astype(BF)
     text_quarters = text_sum.reshape(2, TXT, 2, 2, 256)
@@ -725,61 +800,51 @@
     )
     input_part, scale_grad, shift_grad = mod_back(one_grad[None])
     tokens_grad = pick(self_res_grad.reshape(2, rows, D), core, 0)[None] + input_part
-    mod_own = jnp.concatenate((scale_grad, shift_grad), axis=0)
-    mod_grad = in_order(core, mod_own, swap_core(mod_own), 0)
-    mod_half = pick(mod_grad.reshape(2, 2, 2, 512), core, 2).reshape(2, C_MOD)
-    noise_f = noise.astype(F32)
-    noise_rows = noise_f.reshape(2, 4, 2, 4, 32).transpose(0, 1, 3, 2, 4)[..., None]
-    mod_wg = noise_rows[0] * mod_half[0] + noise_rows[1] * mod_half[1]
-    mod_w = full_one[..., :C_MOD].astype(F32)
-    noise_part = jnp.einsum("ic,zyxrc->izxyr", mod_half, mod_w, precision=HIGHEST_PREC)
-    noise_part = noise_part.reshape(2, D)
-
-    rows_kept, rows_sent = rows_back_kernel(core_id, proj_wg, co_wg)
-    rows_all = join(core, rows_kept, swap_core(rows_sent), 0)
+    mod_grad = jnp.concatenate((scale_grad, shift_grad), axis=1)
+    mod_grad = (mod_grad + swap_seq(mod_grad)).astype(BF)
+    mod_grads = exchange(jnp.broadcast_to(mod_grad, (64, 2 * D)), FSDP)
+    mod_wgrad = jnp.einsum("if,ic->fc", noise_cols, mod_grads, preferred_element_type=F32)
+    noise_parts = jnp.einsum("ic,fc->if", mod_grads, mod_weight, preferred_element_type=F32)
+    noise_grad = exchange(noise_parts, FSDP).reshape(1, D)
+
     gains_wg = jnp.concatenate((gain_two_grad, gain_three_grad), axis=0).astype(BF)
     gains_wg = jnp.pad(
         gains_wg.reshape(2, 64, 16).transpose(1, 0, 2), ((0, 0), (0, 2), (0, C_TEXT - 16))
     )
     text_pack = jnp.concatenate((text_wg.astype(BF).reshape(64, 12, C_TEXT), gains_wg), axis=1)
     text_pack = text_pack.reshape(4, 2, 4, 32, C_TEXT).transpose(0, 2, 1, 3, 4)
-    grads_one = scatter_chips(
-        jnp.concatenate((mod_wg.astype(BF), qkv_wg, cq_wg, text_pack, rows_all), axis=4),
-        xh,
-        TEXT_COLS,
-    )
-
-    shared_cols = C_MOD + C_QKV + C_CQ + C_TEXT
-    grads = jnp.concatenate((grads_one[:, :shared_cols], grads_two[:, :C_UP]), axis=1)
-    grads = grads.reshape(2, 16, shared_cols + C_UP)
-    got = swap_core(pick(grads, 1 - core, 0).astype(BF)).astype(F32)
-    kept_cols = pick(grads, core, 0)
-    by_core = in_order(core, kept_cols, got, 0)
-    at = 0
-    pieces = []
-    for width in (C_MOD, C_QKV, C_CQ, C_TEXT, C_UP):
-        pieces.append(by_core[:, :, at : at + width])
-        at += width
-    mod_g, qkv_g, cq_g, text_g, up_g = pieces
-    mod_wgrad = mod_g.reshape(2, 16, 2, 512).transpose(1, 2, 0, 3).reshape(16, 2 * D)
-    qkv_wgrad = qkv_g.reshape(2, 16, 3, 512).transpose(1, 2, 0, 3).reshape(16, 3, D)
-    cq_wgrad = cq_g.transpose(1, 0, 2).reshape(16, D)
-    text_wgrad = text_g[:, :12].reshape(2, 12, 2, 256).transpose(1, 2, 0, 3).reshape(12, 2, 512)
-    gains_grad = kept_cols[12:14, C_MOD + C_QKV + C_CQ : C_MOD + C_QKV + C_CQ + 16]
-    up_wgrad = up_g.reshape(2, 16, 32, 64).transpose(1, 2, 0, 3).reshape(16, FF)
-    proj_wgrad = rows_as_halves(grads_one[:, shared_cols : shared_cols + C_PROJ])
-    co_wgrad = rows_as_halves(grads_one[:, shared_cols + C_PROJ :])
-    down_g = grads_two[:, C_UP:]
-    down_wgrad = jnp.concatenate((down_g[:, :D], down_g[:, D:]), axis=0)
-
-    small = jnp.concatenate((noise_part[:, None], jnp.pad(text_part, ((0, 0), (0, 0), (0, D - TEXT_W)))), axis=1)
-    small = pick(small, core, 0) + swap_core(pick(small, 1 - core, 0))
-    small = small + swap_seq(small)
+    late_wg = late_kernel(ids, text_pack, qkv_wg, cq_wg, rows_kept, rows_came)
+    late_wg, ff_sc = lax.optimization_barrier((late_wg, ff_sc))
+    late_sc = zy_scatter(late_wg)
+
+    own, far = pick(ff_sc, xh, 0), pick(ff_sc, 1 - xh, 0)
+    ff_g = sum_kernel(own, swap_x(own, xl_pair), swap_x(far, near), swap_x(far, across))
+    up_rows = ff_g[:, :C_UP].reshape(2, 16, C_UP)
+    up_wgrad, down_wgrad = ff_unpack_kernel(
+        ids, pick(up_rows, core, 0), swap_core(pick(up_rows, 1 - core, 0)), ff_g[:, C_UP:]
+    )
+
+    own, far = pick(late_sc, xh, 0), pick(late_sc, 1 - xh, 0)
+    late_g = late_sum_kernel(own, swap_x(own, xl_pair), swap_x(far, near), swap_x(far, across))
+    late_rows = late_g[:, :LATE_ROWS].reshape(2, 16, LATE_ROWS)
+    kept_rows = pick(late_rows, core, 0)
+    came_rows = swap_core(pick(late_rows, 1 - core, 0))
+    qkv_wgrad, cq_wgrad, proj_wgrad, co_wgrad = late_unpack_kernel(
+        ids, kept_rows, came_rows, late_g[:, LATE_ROWS:]
+    )
+    qkv_wgrad = qkv_wgrad.transpose(1, 0, 2)
+    lo, hi = C_QKV, C_QKV + C_TEXT
+    text_both = in_order(core, kept_rows[:, lo:hi], came_rows[:, lo:hi], 0).astype(F32)
+    text_wgrad = text_both[:, :12].reshape(2, 12, 2, 256).transpose(1, 2, 0, 3).reshape(12, 2, 512)
+    gains_grad = kept_rows[12:14, lo : lo + 16].astype(F32)
+
+    text_grad = pick(text_part, core, 0) + swap_core(pick(text_part, 1 - core, 0))
+    text_grad = text_grad + swap_seq(text_grad)
     return (
         block_out,
         tokens_grad,
-        small[:1],
-        small[None, 1:, :TEXT_W],
+        noise_grad,
+        text_grad[None],
         mod_wgrad,
         qkv_wgrad,
         proj_wgrad,

time: 409 us -> 400 us (0.978)
  waiting for transfers between devices: 213 us -> 174 us
  blocking collectives: 0 us -> 20 us
  starting transfers between devices: 34.7 us -> 52.2 us
  Pallas kernels: 67.7 us -> 79.3 us
  local copies, waits for them, and re-layouts: 33.5 us -> 26.1 us
  other arithmetic: 29.3 us -> 22 us
    all_gather x2, waiting for transfers between devices: 86.9 us -> 54.7 us  [gather_chips(): full = lax.all_gather(pair, ('z', 'y'), axis=0, tiled=False)]
    all_to_all x0 -> x3, starting transfers between devices: none -> 20.3 us  [exchange(): return lax.all_to_all(value, axes, 0, 0, tiled=True)]
    all_to_all x0 -> x1, blocking collectives: none -> 20 us  [exchange(): return lax.all_to_all(value, axes, 0, 0, tiled=True)]
    all_to_all x0 -> x3, waiting for transfers between devices: none -> 19.8 us  [exchange(): return lax.all_to_all(value, axes, 0, 0, tiled=True)]
    reduce_scatter x2, waiting for transfers between devices: 72.9 us -> 56.2 us  [zy_scatter(): lax.psum_scatter(full.reshape(D, cols), ('z', 'y'), scatter_dimension=0,...]
    ppermute x9, waiting for transfers between devices: 31.8 us -> 16.9 us  [swap_x(): lax.ppermute(value, RING_X, [p for a, b in pairs for p in ((a, b), (b, a))])]
    pallas_call x10 -> x14, Pallas kernels: 67.7 us -> 79.3 us  [call(): pl.pallas_call(body, out_shape=outs, grid_spec=pltpu.PrefetchScalarGridSp...]
    ppermute x5 -> x6, waiting for transfers between devices: 13 us -> 20.9 us  [swap_seq(): return lax.ppermute(value, 'xl', [(0, 1), (1, 0)])]
  transfers between devices with their start and end apart: 34 -> 38, of which waited for: 17 -> 21; matrix products, arithmetic and copies ran while one was open for 13% -> 9% of each run, Pallas kernels for 13% -> 15%
where the time goes in v3:
time: 400 us; the launch traced here: 392 us
  waiting for transfers between devices  174 us (44%)
  Pallas kernels  79.3 us (20%)
  starting transfers between devices  52.2 us (13%)
  local copies, waits for them, and re-layouts  26.1 us (7%)
  other arithmetic  22 us (6%)
  blocking collectives  20 us (5%)
  between operations  15.7 us (4%)
    pallas_call x14, Pallas kernels, call(): pl.pallas_call(body, out_shape=outs, grid_spec=pltpu.PrefetchScalarGridSp...  79.3 us
    reduce_scatter x2, waiting for transfers between devices, zy_scatter(): lax.psum_scatter(full.reshape(D, cols), ('z', 'y'), scatter_dimension=0,...  56.2 us
    all_gather x2, waiting for transfers between devices, gather_chips(): full = lax.all_gather(pair, ('z', 'y'), axis=0, tiled=False)  54.7 us
    ppermute x6, waiting for transfers between devices, swap_seq(): return lax.ppermute(value, 'xl', [(0, 1), (1, 0)])  20.9 us
    all_to_all x3, starting transfers between devices, exchange(): return lax.all_to_all(value, axes, 0, 0, tiled=True)  20.3 us
    all_to_all x1, blocking collectives, exchange(): return lax.all_to_all(value, axes, 0, 0, tiled=True)  20 us
    all_to_all x3, waiting for transfers between devices, exchange(): return lax.all_to_all(value, axes, 0, 0, tiled=True)  19.8 us
    ppermute x9, waiting for transfers between devices, swap_x(): lax.ppermute(value, RING_X, [p for a, b in pairs for p in ((a, b), (b, a))])  16.9 us
  transfers between devices with their start and end apart: 38, of which 21 were waited for; matrix products, arithmetic and copies ran while one was open for 9% of the time, Pallas kernels for 15%

profile of v3, /device:TPU:1, one launch (start us, length us, event | category | flops | bytes accessed | tf_op | source)
XLA Modules:
  0.0 392.5 jit_solution(5612624987663190743)
XLA Ops:
  18.0 6.8 %collective-permute-done.3 = bf16[32,3584]{1,0:T(8,128)(2,1)S(1)} collective-permute-done((bf16[32,3584]{1,0:T(8,128)(2,1)S(1)}, bf16[32,3584]{1,0:T(8,128)(2,1)S(1)}, u32[]{:S(2)}, u32[]{:S(2)}) %collective-permute-start.3) | collective-permute-done | bytes 229408 | tf_op jit(solution)/shard_map/ppermute | solution.py:625
  27.3 6.1 %collective-permute-done.11 = bf16[32,4096]{1,0:T(8,128)(2,1)S(1)} collective-permute-done((bf16[32,4096]{1,0:T(8,128)(2,1)S(1)}, bf16[32,4096]{1,0:T(8,128)(2,1)S(1)}, u32[]{:S(2)}, u32[]{:S(2)}) %collective-permute-start.11) | collective-permute-done | bytes 262176 | tf_op jit(solution)/shard_map/ppermute | solution.py:625
  34.5 20.0 %all_to_all.40 = bf16[64,1,16]{2,1,0:T(2,128)(2,1)S(1)} all-to-all(bf16[64,1,16]{2,1,0:T(2,128)(2,1)S(1)} %all_to_all.35), channel_id=1, replica_groups=mesh['z'=4,'xh'=2,'y'=4,'core'=2,'xl'=2] {'z','xh','y','core'}, dimensions={0} | all-to-all | bytes 4096 | tf_op jit(solution)/shard_map/all_to_all | solution.py:658
  56.2 4.7 %all-to-all-start.1 = ((f32[64,1,2048]{2,1,0:T(1,128)}), f32[64,1,2048]{2,1,0:T(1,128)S(1)}, u32[]{:S(2)}, u32[]{:S(2)}) async-start(f32[64,1,2048]{2,1,0:T(1,128)} %copy.136), calls=%async_computation.1 | async-start | bytes 1048576 | tf_op jit(solution)/shard_map/all_to_all | solution.py:658
  62.6 12.5 %all-to-all-done.1 = f32[64,1,2048]{2,1,0:T(1,128)S(1)} async-done(((f32[64,1,2048]{2,1,0:T(1,128)}), f32[64,1,2048]{2,1,0:T(1,128)S(1)}, u32[]{:S(2)}, u32[]{:S(2)}) %all-to-all-start.1) | async-done | bytes 524320 | tf_op jit(solution)/shard_map/all_to_all | solution.py:658
  75.9 23.7 %all-gather.5.cloned.1.call-done = bf16[32,32,3584]{2,1,0:T(8,128)(2,1)} async-done(((bf16[2,32,3584]{2,1,0:T(8,128)(2,1)}), bf16[32,32,3584]{2,1,0:T(8,128)(2,1)}) %all-gather.5.cloned.1.call-update) | async-done | bytes 7340048 | tf_op jit(solution)/shard_map/all_gather | solution.py:648
  105.3 4.0 %shard_map.237 = (bf16[256,1024]{1,0:T(8,128)(2,1)}, bf16[256,512]{1,0:T(8,128)(2,1)}, bf16[256,1024]{1,0:T(8,128)(2,1)}) custom-call(bf16[256,1024]{1,0:T(8,128)(2,1)} %bitcast.180, f32[2,1024]{1,0:T(2,128)} %get-tuple-element.151.scale, f32[2,1024]{1,0:T(2,128)} %get-tuple-element.150.shift, bf16[4,4,2,32,3584]{4,3,2,1,0:T(8,128)(2,1)} %bitcast.162, ...), custom_call_target="tpu_custom_call" | custom-call | tf_op jit(solution)/shard_map/pallas_call | solution.py:75
  115.5 7.7 %collective-permute-done.5.kv_far = bf16[256,1024]{1,0:T(8,128)(2,1)} collective-permute-done((bf16[256,1024]{1,0:T(8,128)(2,1)}, bf16[256,1024]{1,0:T(8,128)(2,1)}, u32[]{:S(2)}, u32[]{:S(2)}) %collective-permute-start.5) | collective-permute-done | bytes 524320 | tf_op jit(solution)/shard_map/ppermute | solution.py:621
  123.3 6.0 %shard_map.239 = (bf16[256,512]{1,0:T(8,128)(2,1)}, f32[256,1024]{1,0:T(8,128)}) custom-call(bf16[256,512]{1,0:T(8,128)(2,1)} %get-tuple-element.56.q, bf16[256,1024]{1,0:T(8,128)(2,1)} %get-tuple-element.57.kv, bf16[256,1024]{1,0:T(8,128)(2,1)} %collective-permute-done.5.kv_far, bf16[512,1024]{1,0:T(8,128)(2,1)} %get-tuple-element.58.proj_w), custom_call_target="tpu_custom_call" | custom-call | tf_op jit(solution)/shard_map/pallas_call | solution.py:75
  135.6 5.2 %shard_map.240 = (f32[256,1024]{1,0:T(8,128)}, bf16[256,1024]{1,0:T(8,128)(2,1)}, bf16[256,512]{1,0:T(8,128)(2,1)}, bf16[256,512]{1,0:T(8,128)(2,1)}, f32[256,1024]{1,0:T(8,128)}) custom-call(bf16[256,1024]{1,0:T(8,128)(2,1)} %bitcast.181, f32[256,1024]{1,0:T(8,128)} %get-tuple-element.59.part, f32[256,1024]{1,0:T(8,128)} %collective-permute-done.7.part_far, ...), custom_call_target="tpu_custom_call" | custom-call | tf_op jit(solution)/shard_map/pallas_call | solution.py:75
  141.2 31.0 %all-gather.7.cloned.1.call-done = bf16[32,32,4096]{2,1,0:T(8,128)(2,1)} async-done(((bf16[2,32,4096]{2,1,0:T(8,128)(2,1)}), bf16[32,32,4096]{2,1,0:T(8,128)(2,1)}) %all-gather.7.cloned.1.call-update) | async-done | bytes 8388624 | tf_op jit(solution)/shard_map/all_gather | solution.py:648
  173.2 15.8 %shard_map.241 = (f32[256,1024]{1,0:T(8,128)}, bf16[4,4,2,32,4096]{4,3,2,1,0:T(8,128)(2,1)}, f32[256,1024]{1,0:T(8,128)}, f32[256,1024]{1,0:T(8,128)}) custom-call(f32[256,1024]{1,0:T(8,128)} %get-tuple-element.61.res, f32[256,1024]{1,0:T(8,128)} %get-tuple-element.62.part, f32[256,1024]{1,0:T(8,128)} %copy-done.7, f32[2,1024]{1,0:T(2,128)} %reshape.447.gains, ...), custom_call_target="tpu_custom_call" | custom-call | tf_op jit(solution)/shard_map/pallas_call | solution.py:75
  194.1 7.9 %shard_map.242 = (f32[256,1024]{1,0:T(8,128)}, f32[1,1024]{1,0:T(1,128)}, bf16[512,1024]{1,0:T(8,128)(2,1)}, bf16[4,4,2,32,512]{4,3,2,1,0:T(8,128)(2,1)}, f32[2,8,1024]{2,1,0:T(8,128)}, /*index=5*/f32[256,1024]{1,0:T(8,128)}) custom-call(f32[256,1024]{1,0:T(8,128)} %get-tuple-element.66.part, f32[256,1024]{1,0:T(8,128)} %copy-done.6, ...), custom_call_target="tpu_custom_call" | custom-call | tf_op jit(solution)/shard_map/pallas_call | solution.py:75
  208.4 13.6 %shard_map.243 = (f32[256,1024]{1,0:T(8,128)}, f32[1,1024]{1,0:T(1,128)}, bf16[512,1024]{1,0:T(8,128)(2,1)}, bf16[256,512]{1,0:T(8,128)(2,1)}, f32[256,1024]{1,0:T(8,128)}, /*index=5*/bf16[256,1024]{1,0:T(8,128)(2,1)}) custom-call(f32[256,1024]{1,0:T(8,128)} %get-tuple-element.70.part, f32[256,1024]{1,0:T(8,128)} %copy-done.12, ...), custom_call_target="tpu_custom_call" | custom-call | tf_op jit(solution)/shard_map/pallas_call | solution.py:75
  222.1 3.3 shard_map.245
  232.7 9.1 %collective-permute-done.15.dfar = bf16[256,1024]{1,0:T(8,128)(2,1)S(1)} collective-permute-done((bf16[256,1024]{1,0:T(8,128)(2,1)}, bf16[256,1024]{1,0:T(8,128)(2,1)S(1)}, u32[]{:S(2)}, u32[]{:S(2)}) %collective-permute-start.15) | collective-permute-done | bytes 524320 | tf_op jit(solution)/shard_map/ppermute | solution.py:621
  242.6 6.4 %shard_map.244 = (bf16[4,4,2,32,1536]{4,3,2,1,0:T(8,128)(2,1)}, f32[256,1024]{1,0:T(8,128)}) custom-call(bf16[256,512]{1,0:T(8,128)(2,1)} %get-tuple-element.74.dq, f32[256,1024]{1,0:T(8,128)} %get-tuple-element.75.dkv, bf16[256,1024]{1,0:T(8,128)(2,1)} %copy-done.14, bf16[256,1024]{1,0:T(8,128)(2,1)} %get-tuple-element.77.n1, ...), custom_call_target="tpu_custom_call" | custom-call | tf_op jit(solution)/shard_map/pallas_call | solution.py:75
  249.0 6.5 %shard_map.246 = bf16[4,4,2,32,3584]{4,3,2,1,0:T(8,128)(2,1)} custom-call(s32[4]{0:T(128)} %pad_add_fusion.ids, bf16[4,4,2,32,512]{4,3,2,1,0:T(8,128)(2,1)} %bitcast.184, bf16[4,4,2,32,1536]{4,3,2,1,0:T(8,128)(2,1)} %get-tuple-element.82.qkv, bf16[4,4,2,32,512]{4,3,2,1,0:T(8,128)(2,1)} %get-tuple-element.83.cq, ...), custom_call_target="tpu_custom_call" | custom-call | tf_op jit(solution)/shard_map/pallas_call | solution.py:75
  255.5 17.1 %reduce-scatter.3.cloned.1.call-done = bf16[64,4096]{1,0:T(8,128)(2,1)} async-done(((bf16[1024,4096]{1,0:T(8,128)(2,1)}), bf16[64,4096]{1,0:T(8,128)(2,1)}) %reduce-scatter.3.cloned.1.call-update) | async-done | bytes 524304 | tf_op jit(solution)/shard_map/reduce_scatter | solution.py:663
  288.0 10.5 %all-to-all-start.2 = ((bf16[64,2,1024]{2,1,0:T(2,128)(2,1)}), bf16[64,2,1024]{2,1,0:T(2,128)(2,1)S(1)}, u32[]{:S(2)}, u32[]{:S(2)}) async-start(bf16[64,2,1024]{2,1,0:T(2,128)(2,1)} %reshape.479), calls=%async_computation.2 | async-start | bytes 524288 | tf_op jit(solution)/shard_map/all_to_all | solution.py:658
  302.8 7.3 %all-to-all-done.2 = bf16[64,2,1024]{2,1,0:T(2,128)(2,1)S(1)} async-done(((bf16[64,2,1024]{2,1,0:T(2,128)(2,1)}), bf16[64,2,1024]{2,1,0:T(2,128)(2,1)S(1)}, u32[]{:S(2)}, u32[]{:S(2)}) %all-to-all-start.2) | async-done | bytes 262176 | tf_op jit(solution)/shard_map/all_to_all | solution.py:658
  311.2 5.1 %all-to-all-start.3 = ((f32[64,1,16]{2,1,0:T(1,128)}), f32[64,1,16]{2,1,0:T(1,128)S(1)}, u32[]{:S(2)}, u32[]{:S(2)}) async-start(f32[64,1,16]{2,1,0:T(1,128)} %bitcast.74), calls=%async_computation.3 | async-start | bytes 65536 | tf_op jit(solution)/shard_map/all_to_all | solution.py:658
  321.9 39.1 %reduce-scatter.5.cloned.1.call-done = bf16[64,3584]{1,0:T(8,128)(2,1)} async-done(((bf16[1024,3584]{1,0:T(8,128)(2,1)}), bf16[64,3584]{1,0:T(8,128)(2,1)}) %reduce-scatter.5.cloned.1.call-update) | async-done | bytes 458768 | tf_op jit(solution)/shard_map/reduce_scatter | solution.py:663
  371.7 3.7 collective-permute-done.24.b
  (255 shorter events, 103.5 us)
Async XLA Ops:
  7.2 92.4 %all-gather.5.cloned.1.call-start = ((), (), s32[]{:S(2)}) async-start(), calls=%async_computation.8 | async-start | bytes 7798784 | tf_op jit(solution)/shard_map/all_gather | solution.py:648
  14.1 10.8 %collective-permute-start.4 = (bf16[32,512]{1,0:T(8,128)(2,1)S(1)}, bf16[32,512]{1,0:T(8,128)(2,1)S(1)}, u32[]{:S(2)}, u32[]{:S(2)}) collective-permute-start(bf16[32,512]{1,0:T(8,128)(2,1)S(1)} %pad_maximum_fusion.9), channel_id=1, source_target_pairs={{0,16},{16,0},{1,17},{17,1},{2,18},{18,2},{3,19},{19,3},{4,20},{20... | collective-permute-start | bytes 98312 | tf_op jit(solution)/shard_map/ppermute | solution.py:625
  17.0 7.8 %collective-permute-start.3 = (bf16[32,3584]{1,0:T(8,128)(2,1)S(1)}, bf16[32,3584]{1,0:T(8,128)(2,1)S(1)}, u32[]{:S(2)}, u32[]{:S(2)}) collective-permute-start(bf16[32,3584]{1,0:T(8,128)(2,1)S(1)} %maximum_maximum_fusion), channel_id=1, source_target_pairs={{0,17},{17,0},{1,16},{16,1},{2,19},{19,2},{3,18},{18,3},{4,21},{21... | collective-permute-start | bytes 688136 | tf_op jit(solution)/shard_map/ppermute | solution.py:625
  25.8 146.4 %all-gather.7.cloned.1.call-start = ((), (), s32[]{:S(2)}) async-start(), calls=%async_computation.9 | async-start | bytes 8912896 | tf_op jit(solution)/shard_map/all_gather | solution.py:648
  25.8 7.6 %collective-permute-start.11 = (bf16[32,4096]{1,0:T(8,128)(2,1)S(1)}, bf16[32,4096]{1,0:T(8,128)(2,1)S(1)}, u32[]{:S(2)}, u32[]{:S(2)}) collective-permute-start(bf16[32,4096]{1,0:T(8,128)(2,1)S(1)} %pad_maximum_fusion.3), channel_id=1, source_target_pairs={{0,17},{17,0},{1,16},{16,1},{2,19},{19,2},{3,18},{18,3},{4,21},{21... | collective-permute-start | bytes 786440 | tf_op jit(solution)/shard_map/ppermute | solution.py:625
  56.2 18.8 %all-to-all-start.1 = ((f32[64,1,2048]{2,1,0:T(1,128)}), f32[64,1,2048]{2,1,0:T(1,128)S(1)}, u32[]{:S(2)}, u32[]{:S(2)}) async-start(f32[64,1,2048]{2,1,0:T(1,128)} %copy.136), calls=%async_computation.1 | async-start | bytes 1048576 | tf_op jit(solution)/shard_map/all_to_all | solution.py:658
  61.0 211.7 %reduce-scatter.3.cloned.1.call-start = ((), (), s32[]{:S(2)}) async-start(), calls=%async_computation.6 | async-start | bytes 8912896 | tf_op jit(solution)/shard_map/reduce_scatter | solution.py:663
  61.9 42.0 %collective-permute-start = (bf16[272,1024]{1,0:T(8,128)(2,1)S(1)}, bf16[272,1024]{1,0:T(8,128)(2,1)S(1)}, u32[]{:S(2)}, u32[]{:S(2)}) collective-permute-start(bf16[272,1024]{1,0:T(8,128)(2,1)S(1)} %fusion.8), channel_id=1, source_target_pairs={{0,2},{2,0},{1,3},{3,1},{4,6},{6,4},{5,7},{7,5},{8,10},{10,8},{9,1... | collective-permute-start | bytes 1671176 | tf_op jit(solution)/shard_map/ppermute | solution.py:617
  75.4 27.9 %collective-permute-start.1 = (f32[1,2048]{1,0:T(1,128)S(1)}, f32[1,2048]{1,0:T(1,128)S(1)}, u32[]{:S(2)}, u32[]{:S(2)}) collective-permute-start(f32[1,2048]{1,0:T(1,128)S(1)} %bitcast.216), channel_id=1, source_target_pairs={{0,2},{2,0},{1,3},{3,1},{4,6},{6,4},{5,7},{7,5},{8,10},{10,8},{9,1... | collective-permute-start | bytes 24584 | tf_op jit(solution)/shard_map/ppermute | solution.py:617
  102.6 9.9 %collective-permute-start.6 = (bf16[2,4,2,32,1024]{4,3,2,1,0:T(8,128)(2,1)}, bf16[2,4,2,32,1024]{4,3,2,1,0:T(8,128)(2,1)}, u32[]{:S(2)}, u32[]{:S(2)}) collective-permute-start(bf16[2,4,2,32,1024]{4,3,2,1,0:T(8,128)(2,1)} %get-tuple-element.104), channel_id=1, source_target_pairs={{0,2},{2,0},{1,3},{3,1},{4,6},{6,4},{5,7},{7,5},{8,10},{10,8},{9,1... | collective-permute-start | bytes 3145736 | tf_op jit(solution)/shard_map/ppermute | solution.py:617
  109.3 14.0 %collective-permute-start.5 = (bf16[256,1024]{1,0:T(8,128)(2,1)}, bf16[256,1024]{1,0:T(8,128)(2,1)}, u32[]{:S(2)}, u32[]{:S(2)}) collective-permute-start(bf16[256,1024]{1,0:T(8,128)(2,1)} %get-tuple-element.57.kv), channel_id=1, source_target_pairs={{0,1},{1,0},{2,3},{3,2},{4,5},{5,4},{6,7},{7,6},{8,9},{9,8},{10,11... | collective-permute-start | bytes 1572872 | tf_op jit(solution)/shard_map/ppermute | solution.py:621
  140.8 31.4 %collective-permute-start.10 = (f32[256,1024]{1,0:T(8,128)}, f32[256,1024]{1,0:T(8,128)S(1)}, u32[]{:S(2)}, u32[]{:S(2)}) collective-permute-start(f32[256,1024]{1,0:T(8,128)} %get-tuple-element.62.part), channel_id=1, source_target_pairs={{0,2},{2,0},{1,3},{3,1},{4,6},{6,4},{5,7},{7,5},{8,10},{10,8},{9,1... | collective-permute-start | bytes 3145736 | tf_op jit(solution)/shard_map/ppermute | solution.py:617
  189.0 172.0 %reduce-scatter.5.cloned.1.call-start = ((), (), s32[]{:S(2)}) async-start(), calls=%async_computation.7 | async-start | bytes 7798784 | tf_op jit(solution)/shard_map/reduce_scatter | solution.py:663
  225.3 23.7 %collective-permute-start.22 = (bf16[2,4,2,32,1024]{4,3,2,1,0:T(8,128)(2,1)}, bf16[2,4,2,32,1024]{4,3,2,1,0:T(8,128)(2,1)}, u32[]{:S(2)}, u32[]{:S(2)}) collective-permute-start(bf16[2,4,2,32,1024]{4,3,2,1,0:T(8,128)(2,1)} %get-tuple-element.87), channel_id=1, source_target_pairs={{0,2},{2,0},{1,3},{3,1},{4,6},{6,4},{5,7},{7,5},{8,10},{10,8},{9,1... | collective-permute-start | bytes 3145736 | tf_op jit(solution)/shard_map/ppermute | solution.py:617
  228.1 13.7 %collective-permute-start.15 = (bf16[256,1024]{1,0:T(8,128)(2,1)}, bf16[256,1024]{1,0:T(8,128)(2,1)S(1)}, u32[]{:S(2)}, u32[]{:S(2)}) collective-permute-start(bf16[256,1024]{1,0:T(8,128)(2,1)} %get-tuple-element.76), channel_id=1, source_target_pairs={{0,1},{1,0},{2,3},{3,2},{4,5},{5,4},{6,7},{7,6},{8,9},{9,8},{10,11... | collective-permute-start | bytes 1572872 | tf_op jit(solution)/shard_map/ppermute | solution.py:621
  288.0 22.1 %all-to-all-start.2 = ((bf16[64,2,1024]{2,1,0:T(2,128)(2,1)}), bf16[64,2,1024]{2,1,0:T(2,128)(2,1)S(1)}, u32[]{:S(2)}, u32[]{:S(2)}) async-start(bf16[64,2,1024]{2,1,0:T(2,128)(2,1)} %reshape.479), calls=%async_computation.2 | async-start | bytes 524288 | tf_op jit(solution)/shard_map/all_to_all | solution.py:658
  298.5 17.8 %collective-permute-start.29 = (bf16[32,4096]{1,0:T(8,128)(2,1)S(1)}, bf16[32,4096]{1,0:T(8,128)(2,1)S(1)}, u32[]{:S(2)}, u32[]{:S(2)}) collective-permute-start(bf16[32,4096]{1,0:T(8,128)(2,1)S(1)} %get-tuple-element.110), channel_id=1, source_target_pairs={{0,16},{16,0},{1,17},{17,1},{2,18},{18,2},{3,19},{19,3},{4,20},{20... | collective-permute-start | bytes 786440 | tf_op jit(solution)/shard_map/ppermute | solution.py:625
  301.5 15.0 %collective-permute-start.28 = (bf16[32,4096]{1,0:T(8,128)(2,1)S(1)}, bf16[32,4096]{1,0:T(8,128)(2,1)S(1)}, u32[]{:S(2)}, u32[]{:S(2)}) collective-permute-start(bf16[32,4096]{1,0:T(8,128)(2,1)S(1)} %get-tuple-element.110), channel_id=1, source_target_pairs={{0,17},{17,0},{1,16},{16,1},{2,19},{19,2},{3,18},{18,3},{4,21},{21... | collective-permute-start | bytes 786440 | tf_op jit(solution)/shard_map/ppermute | solution.py:625
  301.5 15.0 %collective-permute-start.27 = (bf16[32,4096]{1,0:T(8,128)(2,1)S(1)}, bf16[32,4096]{1,0:T(8,128)(2,1)S(1)}, u32[]{:S(2)}, u32[]{:S(2)}) collective-permute-start(bf16[32,4096]{1,0:T(8,128)(2,1)S(1)} %get-tuple-element.111.refs_0_), channel_id=1, source_target_pairs={{0,1},{1,0},{16,17},{17,16},{2,3},{3,2},{18,19},{19,18},{4,5},{5,4... | collective-permute-start | bytes 786440 | tf_op jit(solution)/shard_map/ppermute | solution.py:625
  311.2 55.5 %all-to-all-start.3 = ((f32[64,1,16]{2,1,0:T(1,128)}), f32[64,1,16]{2,1,0:T(1,128)S(1)}, u32[]{:S(2)}, u32[]{:S(2)}) async-start(f32[64,1,16]{2,1,0:T(1,128)} %bitcast.74), calls=%async_computation.3 | async-start | bytes 65536 | tf_op jit(solution)/shard_map/all_to_all | solution.py:658
  321.5 47.7 %collective-permute-start.30 = (bf16[16,2048]{1,0:T(8,128)(2,1)S(1)}, bf16[16,2048]{1,0:T(8,128)(2,1)S(1)}, u32[]{:S(2)}, u32[]{:S(2)}) collective-permute-start(bf16[16,2048]{1,0:T(8,128)(2,1)S(1)} %get-tuple-element.122), channel_id=1, source_target_pairs={{0,2},{2,0},{1,3},{3,1},{4,6},{6,4},{5,7},{7,5},{8,10},{10,8},{9,1... | collective-permute-start | bytes 196616 | tf_op jit(solution)/shard_map/ppermute | solution.py:617
  362.1 9.7 %collective-permute-start.25 = (bf16[32,3584]{1,0:T(8,128)(2,1)S(1)}, bf16[32,3584]{1,0:T(8,128)(2,1)S(1)}, u32[]{:S(2)}, u32[]{:S(2)}) collective-permute-start(bf16[32,3584]{1,0:T(8,128)(2,1)S(1)} %get-tuple-element.116), channel_id=1, source_target_pairs={{0,16},{16,0},{1,17},{17,1},{2,18},{18,2},{3,19},{19,3},{4,20},{20... | collective-permute-start | bytes 688136 | tf_op jit(solution)/shard_map/ppermute | solution.py:625
  364.9 10.6 %collective-permute-start.24 = (bf16[32,3584]{1,0:T(8,128)(2,1)S(1)}, bf16[32,3584]{1,0:T(8,128)(2,1)S(1)}, u32[]{:S(2)}, u32[]{:S(2)}) collective-permute-start(bf16[32,3584]{1,0:T(8,128)(2,1)S(1)} %get-tuple-element.116), channel_id=1, source_target_pairs={{0,17},{17,0},{1,16},{16,1},{2,19},{19,2},{3,18},{18,3},{4,21},{21... | collective-permute-start | bytes 688136 | tf_op jit(solution)/shard_map/ppermute | solution.py:625
  365.8 9.7 %collective-permute-start.23 = (bf16[32,3584]{1,0:T(8,128)(2,1)S(1)}, bf16[32,3584]{1,0:T(8,128)(2,1)S(1)}, u32[]{:S(2)}, u32[]{:S(2)}) collective-permute-start(bf16[32,3584]{1,0:T(8,128)(2,1)S(1)} %get-tuple-element.117.own), channel_id=1, source_target_pairs={{0,1},{1,0},{16,17},{17,16},{2,3},{3,2},{18,19},{19,18},{4,5},{5,4... | collective-permute-start | bytes 688136 | tf_op jit(solution)/shard_map/ppermute | solution.py:625
  (48 other events, 258.7 us)
Sparse Core Ops, SparseCore 0:
  25.9 73.6 all-gather.4
  101.7 70.4 all-gather.6
  189.1 83.4 reduce-scatter.2
  276.0 84.9 reduce-scatter.4
